TPU v7x, 32 devices: a whole 2x2x4 slice. The times are simulated.
32 devices in a mesh: dp: 4 (over y, core), row: 2 (over x), col: 4 (over z).
Axes of the slice: x: 2, y: 2, z: 4, core: 2. Of those that a mesh axis runs over, the one named last changes fastest.
Arguments:
- hidden_in: bfloat16 [5120, 2048], P(('dp', 'col'), 'row'), may hold values from -6 to 6
- seq_lengths: int32 [4], P('dp'), may hold values from 512 to 1280, as said below
- gain_attn: bfloat16 [2048], P('row'), may hold values from 0.5 to 1.5
- w_query: bfloat16 [2048, 2048], P('row', 'col'), may hold values from -0.125 to 0.125
- w_key: bfloat16 [2048, 2048], P('row', 'col'), may hold values from -0.125 to 0.125
- w_value: bfloat16 [2048, 2048], P('row', 'col'), may hold values from -0.125 to 0.125
- w_outgate: bfloat16 [2048, 2048], P('row', 'col'), may hold values from -0.125 to 0.125
- rank_down: bfloat16 [2048, 16], P('row'), may hold values from -0.125 to 0.125
- rank_up: bfloat16 [16, 2048], P(None, 'col'), may hold values from -1.5 to 1.5
- decay_bias: float32 [2048], P('col'), may hold values from -1 to 7
- gain_head: bfloat16 [512], P('row'), may hold values from 0.5 to 1.5
- w_output: bfloat16 [2048, 2048], P('col', 'row'), may hold values from -0.1875 to 0.1875
- gain_ffn: bfloat16 [2048], P('row'), may hold values from 0.5 to 1.5
- w_gate: bfloat16 [2048, 5632], P('row', 'col'), may hold values from -0.125 to 0.125
- w_up: bfloat16 [2048, 5632], P('row', 'col'), may hold values from -0.125 to 0.125
- w_down: bfloat16 [5632, 2048], P('col', 'row'), may hold values from -0.109375 to 0.109375
- cotangent: bfloat16 [5120, 2048], P(('dp', 'col'), 'row'), may hold values from -6 to 6
Outputs:
- block_out: bfloat16 [5120, 2048], P(('dp', 'col'), 'row')
- grad_input: float32 [5120, 2048], P(('dp', 'col'), 'row')
- grad_gain_attn: float32 [2048], P('row')
- grad_w_query: float32 [2048, 2048], P('row', 'col')
- grad_w_key: float32 [2048, 2048], P('row', 'col')
- grad_w_value: float32 [2048, 2048], P('row', 'col')
- grad_w_outgate: float32 [2048, 2048], P('row', 'col')
- grad_rank_down: float32 [2048, 16], P('row')
- grad_rank_up: float32 [16, 2048], P(None, 'col')
- grad_decay_bias: float32 [2048], P('col')
- grad_gain_head: float32 [512], P('row')
- grad_w_output: float32 [2048, 2048], P('col', 'row')
- grad_gain_ffn: float32 [2048], P('row')
- grad_w_gate: float32 [2048, 5632], P('row', 'col')
- grad_w_up: float32 [2048, 5632], P('row', 'col')
- grad_w_down: float32 [5632, 2048], P('col', 'row')
Inputs may be any that keep to these rules, and one draw needn't show every extreme that they name: `seq_lengths`: valid tokens of each slot of 1280 positions; every draw has one full slot and one slot of exactly 512 tokens.
All inputs are finite; a program needn't handle non-finite values.
Results may differ from a plain program's by a relative error of at most 0.025.
Values may be sent and summed in bfloat16 or wider, within the bound.
No kernel may reach another device: no remote copies, remote signals or barrier semaphores. Data moves between devices by JAX's collectives and lax.ppermute only.
A program may use at most 256 MiB of HBM per device.

v0:
```python
import math

import jax
import jax.numpy as jnp
from jax import lax
from jax.sharding import PartitionSpec as P

D = 2048
HEAD_K = 512
HEAD_V = 512
BLOCK = 64
SLOT = 1280


EPSILON = 1e-06
HIGHEST = lax.Precision.HIGHEST


def for_sending(x):

    def short(part):
        return part.astype(jnp.bfloat16) if part.dtype == jnp.float32 else part

    return jax.tree.map(short, x)


def product(left, right):
    return jnp.dot(left, right, preferred_element_type=jnp.float32)


def contract_rows(left, right):
    return lax.dot_general(
        left, right, (((0,), (0,)), ((), ())), preferred_element_type=jnp.float32
    )


def contract_cols(left, right):
    return lax.dot_general(
        left, right, (((1,), (1,)), ((), ())), preferred_element_type=jnp.float32
    )


def gla_sequence(queries, key_rows, value_rows, decays):
    block_count = queries.shape[0] // BLOCK
    key_extent = queries.shape[1]
    value_extent = value_rows.shape[1]
    query_blocks = queries.reshape(block_count, BLOCK, key_extent)
    key_blocks = key_rows.reshape(block_count, BLOCK, key_extent)
    value_blocks = value_rows.reshape(block_count, BLOCK, value_extent)
    decay_blocks = decays.reshape(block_count, BLOCK, key_extent)
    running = jnp.cumsum(decay_blocks, axis=1)
    ending = running[:, -1:, :]
    query_fade = query_blocks * jnp.exp(running)
    key_grow = key_blocks * jnp.exp(-running)
    key_final = key_blocks * jnp.exp(ending - running)
    causal = jnp.tril(jnp.ones((BLOCK, BLOCK), jnp.float32))
    scores = jnp.einsum("bik,bjk->bij", query_fade, key_grow, precision=HIGHEST) * causal
    within = jnp.einsum("bij,bjv->biv", scores, value_blocks, precision=HIGHEST)
    updates = jnp.einsum("bjk,bjv->bkv", key_final, value_blocks, precision=HIGHEST)
    fading = jnp.exp(ending[:, 0, :])

    def advance(carried, inputs_now):
        update_now, fade_now = inputs_now
        return (carried * fade_now[:, None] + update_now, carried)

    initial = jnp.zeros((key_extent, value_extent), jnp.float32)
    _, earlier = lax.scan(advance, initial, (updates, fading))
    across = jnp.einsum("bik,bkv->biv", query_fade, earlier, precision=HIGHEST)
    return (within + across).reshape(block_count * BLOCK, value_extent)


def row_total(partial_value):
    return lax.psum(partial_value, "row")


def norm_forward(values, gains, extent):
    summed = row_total(jnp.sum(values * values, axis=1))
    factor = lax.rsqrt(summed / extent + EPSILON)
    return (values * factor[:, None] * gains, factor)


def norm_backward(values, factor, gains, upstream, extent):
    weighted = upstream * gains
    inner_sum = row_total(jnp.sum(weighted * values, axis=1))
    grad_values = (
        factor[:, None] * weighted
        - values * (factor * factor * factor * inner_sum / extent)[:, None]
    )
    grad_gains = jnp.sum(upstream * values * factor[:, None], axis=0)
    return (grad_values, grad_gains)


def gather_tokens(tensor):
    return lax.all_gather(tensor, "col", axis=0, tiled=True)


def share_features(parts):
    return lax.psum_scatter(parts, "row", scatter_dimension=1, tiled=True)


def gather_features(parts):
    return jax.tree.map(
        lambda part, own: part.astype(own.dtype),
        lax.all_gather(for_sending(parts), "row", axis=1, tiled=True),
        parts,
    )


def reduce_tokens(builder, local_rows):
    return lax.psum_scatter(
        builder(jnp.int32(0), local_rows * lax.axis_size("col")),
        "col",
        scatter_dimension=0,
        tiled=True,
    )


def body(
    hidden_in,
    seq_lengths,
    gain_attn,
    w_query,
    w_key,
    w_value,
    w_outgate,
    rank_down,
    rank_up,
    decay_bias,
    gain_head,
    w_output,
    gain_ffn,
    w_gate,
    w_up,
    w_down,
    cotangent,
):
    local_rows = hidden_in.shape[0]
    col_index = lax.axis_index("col")
    row_index = lax.axis_index("row")
    group_rows = local_rows * lax.axis_size("col")
    key_share = HEAD_K // lax.axis_size("row")
    query_scale = 1.0 / math.sqrt(HEAD_K)
    places = jnp.arange(group_rows)
    owners = (places // SLOT)[:, None] == jnp.arange(seq_lengths.shape[0])[None, :]
    limits = jnp.sum(jnp.where(owners, seq_lengths[None, :], 0), axis=1)
    valid_group = (places % SLOT < limits).astype(jnp.float32)
    valid_here = lax.dynamic_slice_in_dim(valid_group, col_index * local_rows, local_rows)
    gain_attn_f = gain_attn.astype(jnp.float32)
    gain_head_f = gain_head.astype(jnp.float32)
    gain_ffn_f = gain_ffn.astype(jnp.float32)
    residual_in = hidden_in.astype(jnp.float32)
    normed_one, factor_one = norm_forward(residual_in, gain_attn_f, D)
    normed_one_low = normed_one.astype(jnp.bfloat16)
    tokens_one = gather_tokens(normed_one_low)
    query_part, key_part, outgate_share = share_features(
        (product(tokens_one, w_query), product(tokens_one, w_key), product(tokens_one, w_outgate))
    )
    value_full, rank_full = lax.psum(
        (product(tokens_one, w_value), product(tokens_one, rank_down)), "row"
    )
    query_low = query_part.astype(jnp.bfloat16)
    key_low = key_part.astype(jnp.bfloat16)
    value_low = value_full.astype(jnp.bfloat16)
    rank_low = rank_full.astype(jnp.bfloat16)
    rank_cols = lax.dynamic_slice_in_dim(rank_up, row_index * key_share, key_share, 1)
    bias_cols = lax.dynamic_slice_in_dim(decay_bias, row_index * key_share, key_share, 0)
    decay_logits = product(rank_low, rank_cols) + bias_cols
    decays = jax.nn.log_sigmoid(decay_logits) / 16.0

    def reshape_slots(tensor):
        return tensor.reshape(seq_lengths.shape[0], SLOT, tensor.shape[1])

    def attend(queries, key_rows, value_rows, decay_rows):
        mixed_slots = jax.vmap(gla_sequence)(
            reshape_slots(queries),
            reshape_slots(key_rows),
            reshape_slots(value_rows),
            reshape_slots(decay_rows),
        )
        return mixed_slots.reshape(group_rows, value_rows.shape[1])

    mixed_part, attend_back = jax.vjp(
        attend,
        query_low.astype(jnp.float32) * query_scale,
        key_low.astype(jnp.float32),
        value_low.astype(jnp.float32),
        decays,
    )
    mixed_share = share_features(mixed_part)
    normed_head, factor_head = norm_forward(mixed_share, gain_head_f, HEAD_V)
    outgate_sig = jax.nn.sigmoid(outgate_share)
    outgate_act = outgate_share * outgate_sig
    gated_share = (normed_head * outgate_act).astype(jnp.bfloat16)
    gated_all = gather_features(gated_share)

    def attn_rows(first_row, row_count):
        return product(gated_all, w_output)

    attn_out = reduce_tokens(attn_rows, local_rows)
    residual_mid = residual_in + attn_out
    normed_two, factor_two = norm_forward(residual_mid, gain_ffn_f, D)
    normed_two_low = normed_two.astype(jnp.bfloat16)
    tokens_two = gather_tokens(normed_two_low)
    gate_pre, up_pre = share_features((product(tokens_two, w_gate), product(tokens_two, w_up)))
    swish_sig = jax.nn.sigmoid(gate_pre)
    swish_out = gate_pre * swish_sig
    hidden_share = (swish_out * up_pre).astype(jnp.bfloat16)
    hidden_all = gather_features(hidden_share)

    def ffn_rows(first_row, row_count):
        return product(hidden_all, w_down)

    ffn_out = reduce_tokens(ffn_rows, local_rows)
    block_out = (valid_here[:, None] * (residual_mid + ffn_out)).astype(jnp.bfloat16)
    upstream = valid_here[:, None] * cotangent.astype(jnp.float32)
    ffn_grad_all = gather_tokens(upstream.astype(jnp.bfloat16))
    hidden_grad = share_features(contract_cols(ffn_grad_all, w_down))
    grad_down = contract_rows(hidden_all, ffn_grad_all)
    swish_slope = swish_sig * (1.0 + gate_pre * (1.0 - swish_sig))
    gate_grad = (hidden_grad * up_pre * swish_slope).astype(jnp.bfloat16)
    up_grad = (hidden_grad * swish_out).astype(jnp.bfloat16)
    gate_grad_all, up_grad_all = gather_features((gate_grad, up_grad))
    grad_gate = contract_rows(tokens_two, gate_grad_all)
    grad_up = contract_rows(tokens_two, up_grad_all)

    def norm_two_rows(first_row, row_count):
        return contract_cols(gate_grad_all, w_gate) + contract_cols(up_grad_all, w_up)

    normed_two_grad = reduce_tokens(norm_two_rows, local_rows)
    mid_part, gain_ffn_grad = norm_backward(
        residual_mid, factor_two, gain_ffn_f, normed_two_grad, D
    )
    mid_grad = upstream + mid_part
    attn_grad_all = gather_tokens(mid_grad.astype(jnp.bfloat16))
    grad_output = contract_rows(gated_all, attn_grad_all)
    gated_grad = share_features(contract_cols(attn_grad_all, w_output))
    head_grad = gated_grad * outgate_act
    outgate_slope = outgate_sig * (1.0 + outgate_share * (1.0 - outgate_sig))
    outgate_grad = (gated_grad * normed_head * outgate_slope).astype(jnp.bfloat16)
    mixed_grad, gain_head_grad = norm_backward(
        mixed_share, factor_head, gain_head_f, head_grad, HEAD_V
    )
    mixed_grad_all, outgate_grad_all = gather_features(
        (mixed_grad.astype(jnp.bfloat16), outgate_grad)
    )
    scaled_grad, key_grad, value_part, decay_grad = attend_back(mixed_grad_all.astype(jnp.float32))
    value_grad = lax.psum(value_part, "row").astype(jnp.bfloat16)
    query_grad = (scaled_grad * query_scale).astype(jnp.bfloat16)
    key_grad_low = key_grad.astype(jnp.bfloat16)
    logit_grad = decay_grad * jax.nn.sigmoid(-decay_logits) / 16.0
    rank_up_part = lax.dot_general(
        rank_low.astype(jnp.float32),
        logit_grad,
        (((0,), (0,)), ((), ())),
        precision=HIGHEST,
        preferred_element_type=jnp.float32,
    )
    rank_up_grad = lax.dynamic_update_slice_in_dim(
        jnp.zeros(rank_up.shape, jnp.float32), rank_up_part, row_index * key_share, 1
    )
    bias_grad = lax.dynamic_update_slice_in_dim(
        jnp.zeros(decay_bias.shape, jnp.float32),
        jnp.sum(logit_grad, axis=0),
        row_index * key_share,
        0,
    )
    rank_term = lax.dot_general(
        logit_grad,
        rank_cols.astype(jnp.float32),
        (((1,), (1,)), ((), ())),
        precision=HIGHEST,
        preferred_element_type=jnp.float32,
    )
    rank_grad = lax.psum(rank_term, ("row", "col")).astype(jnp.bfloat16)
    query_grad_all, key_grad_all = gather_features((query_grad, key_grad_low))
    grad_query = contract_rows(tokens_one, query_grad_all)
    grad_key = contract_rows(tokens_one, key_grad_all)
    grad_value = contract_rows(tokens_one, value_grad)
    grad_outgate = contract_rows(tokens_one, outgate_grad_all)
    grad_rank_down = contract_rows(tokens_one, rank_grad)

    def norm_one_rows(first_row, row_count):
        summed = contract_cols(query_grad_all, w_query)
        summed = summed + contract_cols(key_grad_all, w_key)
        summed = summed + contract_cols(value_grad, w_value)
        summed = summed + contract_cols(outgate_grad_all, w_outgate)
        return summed

    normed_one_grad = reduce_tokens(norm_one_rows, local_rows)
    own_rank = lax.dynamic_slice_in_dim(rank_grad, col_index * local_rows, local_rows, 0)
    normed_one_grad = normed_one_grad + contract_cols(own_rank, rank_down)
    input_part, gain_attn_grad = norm_backward(
        residual_in, factor_one, gain_attn_f, normed_one_grad, D
    )
    grad_input = mid_grad + input_part
    weights_summed = (
        lax.psum(grad_query.astype(jnp.bfloat16), "dp").astype(jnp.float32),
        lax.psum(grad_key.astype(jnp.bfloat16), "dp").astype(jnp.float32),
        lax.psum(grad_value.astype(jnp.bfloat16), "dp").astype(jnp.float32),
        lax.psum(grad_outgate.astype(jnp.bfloat16), "dp").astype(jnp.float32),
        lax.psum(grad_rank_down.astype(jnp.bfloat16), "dp").astype(jnp.float32),
        lax.psum(grad_output.astype(jnp.bfloat16), "dp").astype(jnp.float32),
        lax.psum(grad_gate.astype(jnp.bfloat16), "dp").astype(jnp.float32),
        lax.psum(grad_up.astype(jnp.bfloat16), "dp").astype(jnp.float32),
        lax.psum(grad_down.astype(jnp.bfloat16), "dp").astype(jnp.float32),
    )
    gains_summed = lax.psum((gain_attn_grad, gain_head_grad, gain_ffn_grad), ("dp", "col"))
    decay_summed = (
        lax.psum(rank_up_grad.astype(jnp.bfloat16), ("dp", "row")).astype(jnp.float32),
        lax.psum(bias_grad.astype(jnp.bfloat16), ("dp", "row")).astype(jnp.float32),
    )
    return (
        block_out,
        grad_input,
        gains_summed[0],
        weights_summed[0],
        weights_summed[1],
        weights_summed[2],
        weights_summed[3],
        weights_summed[4],
        decay_summed[0],
        decay_summed[1],
        gains_summed[1],
        weights_summed[5],
        gains_summed[2],
        weights_summed[6],
        weights_summed[7],
        weights_summed[8],
    )


def solution(mesh):
    placed = (
        P(("dp", "col"), "row"),
        P("dp"),
        P("row"),
        P("row", "col"),
        P("row", "col"),
        P("row", "col"),
        P("row", "col"),
        P("row", None),
        P(None, "col"),
        P("col"),
        P("row"),
        P("col", "row"),
        P("row"),
        P("row", "col"),
        P("row", "col"),
        P("col", "row"),
        P(("dp", "col"), "row"),
    )
    return jax.shard_map(
        body,
        mesh=mesh,
        in_specs=placed,
        out_specs=(
            P(("dp", "col"), "row"),
            P(("dp", "col"), "row"),
            P("row"),
            P("row", "col"),
            P("row", "col"),
            P("row", "col"),
            P("row", "col"),
            P("row", None),
            P(None, "col"),
            P("col"),
            P("row"),
            P("col", "row"),
            P("row"),
            P("row", "col"),
            P("row", "col"),
            P("col", "row"),
        ),
        check_vma=False,
    )
```

profile of v0, /device:TPU:10, one launch (start us, length us, event | category | flops | bytes accessed | tf_op | source)
XLA Modules:
  0.0 2066.6 jit_solution(14009256386679125751)
XLA Ops:
  17.2 54.2 %all-gather.13.cloned.1.call-done = bf16[1280,1024]{1,0:T(8,128)(2,1)} async-done(((bf16[320,1024]{1,0:T(8,128)(2,1)}), bf16[1280,1024]{1,0:T(8,128)(2,1)}) %all-gather.13.cloned.1.call-update) | async-done | bytes 2621456 | tf_op jit(solution)/shard_map/all_gather | solution.py:94
  89.1 113.6 %all-reduce.10 = (bf16[1280,16]{0,1:T(8,128)(2,1)}, bf16[1280,512]{1,0:T(8,128)(2,1)}) all-reduce(f32[1280,16]{0,1:T(8,128)S(1)} %fusion.77, f32[1280,512]{1,0:T(8,128)} %fusion.79), channel_id=1, replica_groups=mesh['dp'=4,'row'=2,'col'=4] {'row'}, use_global_device_ids=true, to_apply=%region_3.4 | all-reduce | flops 675840 | bytes 4055040 | tf_op jit(solution)/shard_map/psum | solution.py:158
  226.5 51.8 %while.34 = (s32[]{:T(128)}, f32[1,256,512]{2,1,0:T(8,128)S(1)}, f32[20,1,256,512]{3,2,1,0:T(8,128)}, f32[20,1,256,1]{2,3,1,0:T(1,128)}, f32[20,1,256]{2,1,0:T(1...) while((s32[]{:T(128)}, f32[1,256,512]{2,1,0:T(8,128)S(1)}, ...), condition=%wide.region_8.9_spmd.clone, body=%wide.region_7.8_spmd.clone.sunk | while | flops 524291 | bytes 2627688 | solution.py:67
  283.5 12.0 fusion.10
  301.8 31.7 %reduce-scatter.17.cloned.1.call-done = f32[1280,256]{1,0:T(8,128)} async-done(((f32[1280,512]{1,0:T(8,128)}), f32[1280,256]{1,0:T(8,128)}) %reduce-scatter.17.cloned.1.call-update) | async-done | bytes 1310736 | tf_op jit(solution)/shard_map/reduce_scatter | solution.py:98
  340.1 33.8 %reduce-scatter.19.cloned.1.call-done = f32[1280,256]{1,0:T(8,128)} async-done(((f32[1280,512]{1,0:T(8,128)}), f32[1280,256]{1,0:T(8,128)}) %reduce-scatter.19.cloned.1.call-update) | async-done | bytes 1310736 | tf_op jit(solution)/shard_map/reduce_scatter | solution.py:98
  376.9 24.3 %all-gather.15.cloned.1.call-done = bf16[1280,512]{1,0:T(8,128)(2,1)} async-done(((bf16[1280,256]{1,0:T(8,128)(2,1)}), bf16[1280,512]{1,0:T(8,128)(2,1)}) %all-gather.15.cloned.1.call-update) | async-done | bytes 1310736 | tf_op jit(solution)/shard_map/all_gather | solution.py:104
  411.6 90.0 %reduce-scatter.21.cloned.1.call-done = f32[320,1024]{1,0:T(8,128)} async-done(((f32[1280,1024]{1,0:T(8,128)}), f32[320,1024]{1,0:T(8,128)}) %reduce-scatter.21.cloned.1.call-update) | async-done | bytes 1310736 | tf_op jit(solution)/shard_map/reduce_scatter | solution.py:110
  512.9 44.4 %all-gather.21.cloned.1.call-done = bf16[1280,1024]{1,0:T(8,128)(2,1)} async-done(((bf16[320,1024]{1,0:T(8,128)(2,1)}), bf16[1280,1024]{1,0:T(8,128)(2,1)}) %all-gather.21.cloned.1.call-update) | async-done | bytes 2621456 | tf_op jit(solution)/shard_map/all_gather | solution.py:94
  566.8 46.3 %all-gather.17.cloned.1.call-done = bf16[1280,1024]{1,0:T(8,128)(2,1)} async-done(((bf16[320,1024]{1,0:T(8,128)(2,1)}), bf16[1280,1024]{1,0:T(8,128)(2,1)}) %all-gather.17.cloned.1.call-update) | async-done | bytes 2621456 | tf_op jit(solution)/shard_map/all_gather | solution.py:94
  631.8 70.1 %reduce-scatter.29.cloned.1.call-done = f32[1280,704]{0,1:T(8,128)} async-done(((f32[1280,1408]{0,1:T(8,128)}), f32[1280,704]{0,1:T(8,128)}) %reduce-scatter.29.cloned.1.call-update) | async-done | bytes 3604496 | tf_op jit(solution)/shard_map/reduce_scatter | solution.py:98
  701.9 89.5 %reduce-scatter.23.cloned.1.call-done = f32[1280,704]{0,1:T(8,128)} async-done(((f32[1280,1408]{0,1:T(8,128)}), f32[1280,704]{0,1:T(8,128)}) %reduce-scatter.23.cloned.1.call-update) | async-done | bytes 3604496 | tf_op jit(solution)/shard_map/reduce_scatter | solution.py:98
  791.4 89.2 %reduce-scatter.25.cloned.1.call-done = f32[1280,704]{0,1:T(8,128)} async-done(((f32[1280,1408]{0,1:T(8,128)}), f32[1280,704]{0,1:T(8,128)}) %reduce-scatter.25.cloned.1.call-update) | async-done | bytes 3604496 | tf_op jit(solution)/shard_map/reduce_scatter | solution.py:98
  888.6 48.9 %all-gather.23.cloned.1.call-done = bf16[1280,1408]{0,1:T(8,128)(2,1)} async-done(((bf16[1280,704]{0,1:T(8,128)(2,1)}), bf16[1280,1408]{0,1:T(8,128)(2,1)}) %all-gather.23.cloned.1.call-update) | async-done | bytes 3604496 | tf_op jit(solution)/shard_map/all_gather | solution.py:104
  945.6 44.1 %all-gather.25.cloned.1.call-done = bf16[1280,1408]{0,1:T(8,128)(2,1)} async-done(((bf16[1280,704]{0,1:T(8,128)(2,1)}), bf16[1280,1408]{0,1:T(8,128)(2,1)}) %all-gather.25.cloned.1.call-update) | async-done | bytes 3604496 | tf_op jit(solution)/shard_map/all_gather | solution.py:104
  989.7 11.2 convolution_add_fusion
  1001.0 40.9 %all-gather.19.cloned.1.call-done = bf16[1280,1408]{0,1:T(8,128)(2,1)} async-done(((bf16[1280,704]{0,1:T(8,128)(2,1)}), bf16[1280,1408]{0,1:T(8,128)(2,1)}) %all-gather.19.cloned.1.call-update) | async-done | bytes 3604496 | tf_op jit(solution)/shard_map/all_gather | solution.py:104
  1050.0 89.4 %reduce-scatter.31.cloned.1.call-done = f32[320,1024]{1,0:T(8,128)} async-done(((f32[1280,1024]{1,0:T(8,128)}), f32[320,1024]{1,0:T(8,128)}) %reduce-scatter.31.cloned.1.call-update) | async-done | bytes 1310736 | tf_op jit(solution)/shard_map/reduce_scatter | solution.py:110
  1146.8 89.8 %reduce-scatter.27.cloned.1.call-done = f32[320,1024]{1,0:T(8,128)} async-done(((f32[1280,1024]{1,0:T(8,128)}), f32[320,1024]{1,0:T(8,128)}) %reduce-scatter.27.cloned.1.call-update) | async-done | bytes 1310736 | tf_op jit(solution)/shard_map/reduce_scatter | solution.py:110
  1240.0 53.6 %all-gather.27.cloned.1.call-done = bf16[1280,1024]{1,0:T(8,128)(2,1)} async-done(((bf16[320,1024]{1,0:T(8,128)(2,1)}), bf16[1280,1024]{1,0:T(8,128)(2,1)}) %all-gather.27.cloned.1.call-update) | async-done | bytes 2621456 | tf_op jit(solution)/shard_map/all_gather | solution.py:94
  1313.9 22.2 %reduce-scatter.33.cloned.1.call-done = f32[1280,256]{1,0:T(8,128)} async-done(((f32[1280,512]{1,0:T(8,128)}), f32[1280,256]{1,0:T(8,128)}) %reduce-scatter.33.cloned.1.call-update) | async-done | bytes 1310736 | tf_op jit(solution)/shard_map/reduce_scatter | solution.py:98
  1359.0 12.8 all-gather.29.cloned.1.call-done
  1400.5 136.7 %while.35 = (s32[]{:T(128)}, f32[1,256,512]{2,1,0:T(8,128)S(1)}, f32[20,1,256,512]{3,2,1,0:T(8,128)}, f32[20,1,256]{2,1,0:T(1,128)S(1)}, f32[20,1,256,512]{2,3,0...) while((s32[]{:T(128)}, f32[1,256,512]{2,1,0:T(8,128)S(1)}, ...), condition=%wide.region_28.29_spmd.clone, body=%wide.region_26.28_spmd.clone.sunk | while | flops 786180 | bytes 5249168 | solution.py:67
  1537.3 10.9 fusion.50
  1565.6 79.5 %all-reduce.11 = bf16[1280,512]{1,0:T(8,128)(2,1)} all-reduce(f32[1280,512]{1,0:T(8,128)} %bitcast.223), channel_id=1, replica_groups=mesh['dp'=4,'row'=2,'col'=4] {'row'}, use_global_device_ids=true, to_apply=%region_29.30 | all-reduce | flops 655360 | bytes 3932160 | tf_op jit(solution)/shard_map/psum | solution.py:247
  1656.8 12.7 all-gather.31.cloned.1.call-done
  1691.6 24.8 %all-reduce.3 = (bf16[16,512]{1,0:T(8,128)(2,1)S(1)}, bf16[512]{0:T(512)(128)(2,1)S(1)}) all-reduce(bf16[16,512]{1,0:T(8,128)(2,1)S(1)} %convolution_dynamic-update-slice_fusion, bf16[512]{0:T(512)(128)(2,1)S(1)} %dynamic_update_slice.34), channel_id=1, replica_groups=mesh['dp'=4,'row'=2,'col'=4] {'dp','row'}, use_global_device_ids=true, to_apply=%region_43.44 | all-reduce | flops 8704 | bytes 34816 | tf_op jit(solution)/shard_map/psum | solution.py:309
  1718.3 33.1 %psum.176 = bf16[1280,16]{0,1:T(8,128)(2,1)S(1)} all-reduce(f32[1280,16]{0,1:T(8,128)S(1)} %fusion.60), channel_id=1, replica_groups=mesh['dp'=4,'row'=2,'col'=4] {'row','col'}, use_global_device_ids=true, to_apply=%region_33.34 | all-reduce | flops 20480 | bytes 122880 | tf_op jit(solution)/shard_map/psum | solution.py:274
  1753.7 12.6 psum.183
  1766.9 152.9 %all-reduce.9.cloned.1.call-done = (bf16[1024,512]{1,0:T(8,128)(2,1)}, bf16[1024,512]{1,0:T(8,128)(2,1)}, bf16[1024,512]{1,0:T(8,128)(2,1)}, bf16[1024,512]{1,0:...) async-done(((bf16[1024,512]{1,0:T(8,128)(2,1)}, bf16[1024,512]{1,0:T(8,128)(2,1)}, ...) | async-done | bytes 13893648 | tf_op jit(solution)/shard_map/psum | solution.py:297
  1939.0 77.1 %reduce-scatter.35.cloned.1.call-done = f32[320,1024]{1,0:T(8,128)} async-done(((f32[1280,1024]{1,0:T(8,128)}), f32[320,1024]{1,0:T(8,128)}) %reduce-scatter.35.cloned.1.call-update) | async-done | bytes 1310736 | tf_op jit(solution)/shard_map/reduce_scatter | solution.py:110
  2024.1 32.3 %all-reduce.1 = (f32[1024]{0:T(1024)}, f32[256]{0:T(256)}, f32[1024]{0:T(1024)}) all-reduce(f32[1024]{0:T(1024)S(1)} %get-tuple-element.257, f32[256]{0:T(256)S(1)} %copy-done.72, f32[1024]{0:T(1024)S(1)} %copy-done.67), channel_id=1, replica_groups=mesh['dp'=4,'row'=2,'col'=4] {'dp','col'}, use_global_device_ids=true, to_apply=%region_37.38 | all-reduce | flops 2304 | bytes 18432 | tf_op jit(solution)/shard_map/psum | solution.py:307
  (522 shorter events, 501.7 us)
Async XLA Ops:
  7.2 605.9 %copy-start = (bf16[1024,1408]{1,0:T(8,128)(2,1)S(1)}, bf16[1024,1408]{1,0:T(8,128)(2,1)}, u32[]{:S(2)}) copy-start(bf16[1024,1408]{1,0:T(8,128)(2,1)} %param.34) | copy-start | bytes 8650756
  7.2 64.2 %all-gather.13.cloned.1.call-start = ((), (), s32[]{:S(2)}) async-start(), calls=%async_computation.12 | async-start | bytes 3276800 | tf_op jit(solution)/shard_map/all_gather | solution.py:94
  17.1 190.3 %reduce-scatter.13.cloned.1.call-start = ((), (), s32[]{:S(2)}) async-start(), calls=%async_computation.13 | async-start | bytes 3932160 | tf_op jit(solution)/shard_map/reduce_scatter | solution.py:98
  76.5 135.5 %reduce-scatter.15.cloned.1.call-start = ((), (), s32[]{:S(2)}) async-start(), calls=%async_computation.14 | async-start | bytes 3932160 | tf_op jit(solution)/shard_map/reduce_scatter | solution.py:98
  81.6 251.9 %reduce-scatter.17.cloned.1.call-start = ((), (), s32[]{:S(2)}) async-start(), calls=%async_computation.15 | async-start | bytes 3932160 | tf_op jit(solution)/shard_map/reduce_scatter | solution.py:98
  82.3 196.0 %copy-start.48 = (f32[64,64]{1,0:T(8,128)}, f32[64,64]{1,0:T(8,128)S(1)}, u32[]{:S(2)}) copy-start(f32[64,64]{1,0:T(8,128)S(1)} %fusion.52) | copy-start | bytes 49156
  295.5 78.3 %reduce-scatter.19.cloned.1.call-start = ((), (), s32[]{:S(2)}) async-start(), calls=%async_computation.16 | async-start | bytes 3932160 | tf_op jit(solution)/shard_map/reduce_scatter | solution.py:98
  301.1 100.1 %all-gather.15.cloned.1.call-start = ((), (), s32[]{:S(2)}) async-start(), calls=%async_computation.17 | async-start | bytes 1966080 | tf_op jit(solution)/shard_map/all_gather | solution.py:104
  376.8 124.8 %reduce-scatter.21.cloned.1.call-start = ((), (), s32[]{:S(2)}) async-start(), calls=%async_computation.18 | async-start | bytes 6553600 | tf_op jit(solution)/shard_map/reduce_scatter | solution.py:110
  406.7 150.5 %all-gather.21.cloned.1.call-start = ((), (), s32[]{:S(2)}) async-start(), calls=%async_computation.24 | async-start | bytes 3276800 | tf_op jit(solution)/shard_map/all_gather | solution.py:94
  410.3 202.8 %all-gather.17.cloned.1.call-start = ((), (), s32[]{:S(2)}) async-start(), calls=%async_computation.19 | async-start | bytes 3276800 | tf_op jit(solution)/shard_map/all_gather | solution.py:94
  512.8 189.1 %reduce-scatter.29.cloned.1.call-start = ((), (), s32[]{:S(2)}) async-start(), calls=%async_computation.25 | async-start | bytes 10813440 | tf_op jit(solution)/shard_map/reduce_scatter | solution.py:98
  566.7 224.7 %reduce-scatter.23.cloned.1.call-start = ((), (), s32[]{:S(2)}) async-start(), calls=%async_computation.20 | async-start | bytes 10813440 | tf_op jit(solution)/shard_map/reduce_scatter | solution.py:98
  621.0 259.6 %reduce-scatter.25.cloned.1.call-start = ((), (), s32[]{:S(2)}) async-start(), calls=%async_computation.21 | async-start | bytes 10813440 | tf_op jit(solution)/shard_map/reduce_scatter | solution.py:98
  631.8 305.8 %all-gather.23.cloned.1.call-start = ((), (), s32[]{:S(2)}) async-start(), calls=%async_computation.26 | async-start | bytes 5406720 | tf_op jit(solution)/shard_map/all_gather | solution.py:104
  887.3 102.5 %all-gather.25.cloned.1.call-start = ((), (), s32[]{:S(2)}) async-start(), calls=%async_computation.27 | async-start | bytes 5406720 | tf_op jit(solution)/shard_map/all_gather | solution.py:104
  887.8 154.1 %all-gather.19.cloned.1.call-start = ((), (), s32[]{:S(2)}) async-start(), calls=%async_computation.22 | async-start | bytes 5406720 | tf_op jit(solution)/shard_map/all_gather | solution.py:104
  888.4 251.0 %reduce-scatter.31.cloned.1.call-start = ((), (), s32[]{:S(2)}) async-start(), calls=%async_computation.28 | async-start | bytes 6553600 | tf_op jit(solution)/shard_map/reduce_scatter | solution.py:110
  1001.0 235.6 %reduce-scatter.27.cloned.1.call-start = ((), (), s32[]{:S(2)}) async-start(), calls=%async_computation.23 | async-start | bytes 6553600 | tf_op jit(solution)/shard_map/reduce_scatter | solution.py:110
  1050.0 186.6 %copy-start.34 = (bf16[320,1024]{1,0:T(8,128)(2,1)S(1)}, bf16[320,1024]{1,0:T(8,128)(2,1)}, u32[]{:S(2)}) copy-start(bf16[320,1024]{1,0:T(8,128)(2,1)} %param.37) | copy-start | bytes 1966084
  1050.0 186.6 %copy-start.62 = (f32[320]{0:T(512)S(1)}, f32[320]{0:T(512)}, u32[]{:S(2)}) copy-start(f32[320]{0:T(512)} %copy-done.61) | copy-start | bytes 3844
  1050.0 243.6 %all-gather.27.cloned.1.call-start = ((), (), s32[]{:S(2)}) async-start(), calls=%async_computation.29 | async-start | bytes 3276800 | tf_op jit(solution)/shard_map/all_gather | solution.py:94
  1240.0 96.2 %reduce-scatter.33.cloned.1.call-start = ((), (), s32[]{:S(2)}) async-start(), calls=%async_computation.30 | async-start | bytes 3932160 | tf_op jit(solution)/shard_map/reduce_scatter | solution.py:98
  1298.7 73.1 %all-gather.29.cloned.1.call-start = ((), (), s32[]{:S(2)}) async-start(), calls=%async_computation.31 | async-start | bytes 1966080 | tf_op jit(solution)/shard_map/all_gather | solution.py:104
  1347.5 301.6 %all-gather.35.cloned.1.call-start = ((), (), s32[]{:S(2)}) async-start(), calls=%async_computation.34 | async-start | bytes 1966080 | tf_op jit(solution)/shard_map/all_gather | solution.py:104
  1358.5 294.4 %all-gather.33.cloned.1.call-start = ((), (), s32[]{:S(2)}) async-start(), calls=%async_computation.33 | async-start | bytes 1966080 | tf_op jit(solution)/shard_map/all_gather | solution.py:104
  1400.5 136.8 %copy-start.4 = (f32[1280,256]{1,0:T(8,128)S(1)}, f32[1280,256]{1,0:T(8,128)}, u32[]{:S(2)}) copy-start(f32[1280,256]{1,0:T(8,128)} %copy-done.3) | copy-start | bytes 3932164
  1400.5 136.8 %copy-start.7 = (f32[1,20,64,256]{3,2,1,0:T(8,128)S(1)}, f32[1,20,64,256]{3,2,1,0:T(8,128)}, u32[]{:S(2)}) copy-start(f32[1,20,64,256]{3,2,1,0:T(8,128)} %copy-done.5) | copy-start | bytes 3932164
  1400.5 136.8 %copy-start.47 = (f32[1,20,1,256]{3,1,2,0:T(8,128)S(1)}, f32[1,20,1,256]{3,1,2,0:T(8,128)}, u32[]{:S(2)}) copy-start(f32[1,20,1,256]{3,1,2,0:T(8,128)} %copy-done.46) | copy-start | bytes 61444
  1565.6 103.9 %all-gather.31.cloned.1.call-start = ((), (), s32[]{:S(2)}) async-start(), calls=%async_computation.32 | async-start | bytes 1966080 | tf_op jit(solution)/shard_map/all_gather | solution.py:104
  1645.2 274.7 %all-reduce.9.cloned.1.call-start = ((), (), s32[]{:S(2)}) async-start(), calls=%async_computation.36 | async-start | bytes 27787264 | tf_op jit(solution)/shard_map/psum | solution.py:297
  1673.4 342.7 %reduce-scatter.35.cloned.1.call-start = ((), (), s32[]{:S(2)}) async-start(), calls=%async_computation.35 | async-start | bytes 6553600 | tf_op jit(solution)/shard_map/reduce_scatter | solution.py:110
  (76 other events, 1815.1 us)
Sparse Core Ops, SparseCore 0:
  17.2 54.1 all-gather.12
  76.6 55.0 reduce-scatter.12
  134.6 66.7 reduce-scatter.14
  295.7 37.7 reduce-scatter.16
  336.2 37.5 reduce-scatter.18
  377.0 24.2 all-gather.14
  406.9 94.6 reduce-scatter.20
  503.7 53.5 all-gather.20
  559.4 53.5 all-gather.16
  615.2 86.6 reduce-scatter.28
  704.3 87.0 reduce-scatter.22
  793.6 86.9 reduce-scatter.24
  887.4 50.1 all-gather.22
  939.6 50.0 all-gather.24
  991.8 50.0 all-gather.18
  1044.7 94.6 reduce-scatter.30
  1142.3 94.2 reduce-scatter.26
  1240.1 53.5 all-gather.26
  1298.8 37.2 reduce-scatter.32
  1347.6 24.1 all-gather.28
  1373.9 24.2 all-gather.34
  1565.7 38.3 all-gather.32
  1645.3 24.2 all-gather.30
  1673.7 246.0 all-reduce.8
  1922.2 93.9 reduce-scatter.34
where the time goes:
time: 2080 us; the launch traced here: 2070 us
  waiting for transfers between devices  1220 us (59%)
  blocking collectives  326 us (16%)
  matrix products  222 us (11%)
  other arithmetic  154 us (7%)
  local copies, waits for them, and re-layouts  126 us (6%)
    reduce_scatter x4, waiting for transfers between devices, reduce_tokens(): lax.psum_scatter(builder(jnp.int32(0), local_rows * lax.axis_size('col'))...  346 us
    reduce_scatter x8, waiting for transfers between devices, share_features(): return lax.psum_scatter(parts, 'row', scatter_dimension=1, tiled=True)  337 us
    all_gather x4, waiting for transfers between devices, gather_tokens(): return lax.all_gather(tensor, 'col', axis=0, tiled=True)  199 us
    all_gather x8, waiting for transfers between devices, gather_features(): lax.all_gather(for_sending(parts), 'row', axis=1, tiled=True)  184 us
    psum x1, waiting for transfers between devices, body(): lax.psum(grad_query.astype(jnp.bfloat16), 'dp').astype(jnp.float32)  153 us
    psum x1, blocking collectives, body(): lax.psum((product(tokens_one, w_value), product(tokens_one, rank_down)),...  114 us
    dynamic_slice x80, local copies, waits for them, and re-layouts, gla_sequence(): _, earlier = lax.scan(advance, initial, (updates, fading))  91.4 us
    psum x1, blocking collectives, body(): value_grad = lax.psum(value_part, 'row').astype(jnp.bfloat16)  79.5 us
  transfers between devices with their start and end apart: 25, of which 21 were waited for; matrix products, arithmetic and copies ran while one was open for 17% of the time, Pallas kernels for 0%

commit v1 on v0

v1 whole, which is shorter than its diff:
```python
import math

import jax
import jax.numpy as jnp
from jax import lax
from jax.experimental import pallas as pl
from jax.experimental.pallas import tpu as pltpu
from jax.sharding import PartitionSpec as P

HEAD_K = 512
HEAD_V = 512
SLOT = 1280
EPSILON = 1e-06
HIGHEST = lax.Precision.HIGHEST
HIGH = lax.Precision.HIGH
F32 = jnp.float32
BF16 = jnp.bfloat16

NN = (((1,), (0,)), ((), ()))
NT = (((1,), (1,)), ((), ()))
TN = (((0,), (0,)), ((), ()))


def dot(left, right, dims, precision=None):
    return lax.dot_general(left, right, dims, precision=precision, preferred_element_type=F32)


def split(x):
    high = x.astype(BF16)
    return (high, (x - high.astype(F32)).astype(BF16))


def split_three(x):
    high = x.astype(BF16)
    rest = x - high.astype(F32)
    middle = rest.astype(BF16)
    return (high, middle, (rest - middle.astype(F32)).astype(BF16))


def dot_pair(left, right, dims):
    return (
        dot(left[0], right[0], dims) + dot(left[0], right[1], dims) + dot(left[1], right[0], dims)
    )


def dot_left(left, right, dims):
    return dot(left[0], right, dims) + dot(left[1], right, dims)


def dot_right(left, right, dims):
    return dot(left, right[0], dims) + dot(left, right[1], dims)


def lower_mask(size):
    rows = lax.broadcasted_iota(jnp.int32, (size, size), 0)
    cols = lax.broadcasted_iota(jnp.int32, (size, size), 1)
    return rows >= cols


def block_factors(q_ref, k_ref, decay_ref):
    size = q_ref.shape[0]
    causal = lower_mask(size)
    ones = jnp.where(causal, 1.0, 0.0).astype(BF16)
    parts = split_three(decay_ref[...])
    running = dot(ones, parts[0], NN) + dot(ones, parts[1], NN) + dot(ones, parts[2], NN)
    ending = running[size - 1 :, :]
    grow = jnp.exp(running)
    shrink = jnp.exp(-running)
    last = jnp.exp(ending - running)
    scale = 1.0 / math.sqrt(HEAD_K)
    keys = k_ref[...].astype(F32)
    query_fade = q_ref[...].astype(F32) * scale * grow
    return (causal, ones, ending, grow, shrink, last, query_fade, keys * shrink, keys * last)


def forward_kernel(
    q_ref, k_ref, v_ref, decay_ref, mixed_ref, faded_ref, state_ref, before_ref, carried, total
):
    @pl.when(pl.program_id(0) == 0)
    def _():
        carried[...] = jnp.zeros_like(carried)
        total[...] = jnp.zeros_like(total)

    causal, _, ending, _, _, _, query_fade, key_grow, key_final = block_factors(
        q_ref, k_ref, decay_ref
    )
    values = v_ref[...]
    state = carried[...]
    before = total[...]
    state_ref[0] = state
    before_ref[0] = before
    query_parts = split(query_fade)
    scores = jnp.where(causal, dot_pair(query_parts, split(key_grow), NT), 0.0)
    mixed_ref[...] = dot_left(split(scores), values, NN) + dot_pair(query_parts, split(state), NT)
    faded_ref[...] = query_fade * jnp.exp(before[:1, :])
    carried[...] = state * jnp.exp(ending) + dot_right(values, split(key_final), TN)
    total[...] = before + ending


def state_kernel(k_ref, v_ref, decay_ref, out_ref, carried):
    @pl.when(pl.program_id(0) == 0)
    def _():
        carried[...] = jnp.zeros_like(carried)

    _, _, ending, _, _, _, _, _, key_final = block_factors(k_ref, k_ref, decay_ref)
    state = carried[...] * jnp.exp(ending) + dot_right(v_ref[...], split(key_final), TN)
    carried[...] = state
    out_ref[...] = state


def backward_kernel(
    q_ref,
    k_ref,
    v_ref,
    decay_ref,
    grad_ref,
    state_ref,
    before_ref,
    entry_ref,
    exit_ref,
    query_out,
    key_out,
    value_out,
    decay_out,
    carried,
):
    @pl.when(pl.program_id(0) == 0)
    def _():
        carried[...] = exit_ref[...]

    causal, ones, ending, grow, shrink, last, query_fade, key_grow, key_final = block_factors(
        q_ref, k_ref, decay_ref
    )
    values = v_ref[...]
    state = state_ref[0] + jnp.exp(before_ref[0][:1, :]) * entry_ref[...]
    state_grad = carried[...]
    query_parts = split(query_fade)
    key_parts = split(key_grow)
    grad_parts = split(grad_ref[...])
    carry_parts = split(state_grad)
    scores = jnp.where(causal, dot_pair(query_parts, key_parts, NT), 0.0)
    score_grad = jnp.where(causal, dot_left(grad_parts, values, NT), 0.0)
    score_parts = split(score_grad)
    fade_grad = dot_pair(score_parts, key_parts, NN) + dot_pair(grad_parts, split(state), NN)
    grow_grad = dot_pair(score_parts, query_parts, TN)
    final_grad = dot_right(values, carry_parts, NN)
    value_out[...] = (
        dot_pair(split(scores), grad_parts, TN) + dot_pair(split(key_final), carry_parts, NT)
    ).astype(BF16)
    fading = jnp.exp(ending)
    carried[...] = fading * state_grad + dot_pair(grad_parts, query_parts, TN)
    query_out[...] = (fade_grad * grow * (1.0 / math.sqrt(HEAD_K))).astype(BF16)
    key_out[...] = (grow_grad * shrink + final_grad * last).astype(BF16)
    ended = final_grad * key_final
    running_grad = fade_grad * query_fade - grow_grad * key_grow - ended
    end_grad = jnp.sum(ended, axis=0, keepdims=True) + fading * jnp.sum(
        state_grad * state, axis=0, keepdims=True
    )
    parts = split_three(running_grad)
    decay_out[...] = (
        dot(ones, parts[0], TN) + dot(ones, parts[1], TN) + dot(ones, parts[2], TN) + end_grad
    )


def block_of(rows):
    return 64 if rows % 64 == 0 else 32


def row_spec(block, width, count, backward):
    if backward:
        return pl.BlockSpec((block, width), lambda b: (count - 1 - b, 0))
    return pl.BlockSpec((block, width), lambda b: (b, 0))


def cube_spec(height, width, count, backward):
    if backward:
        return pl.BlockSpec((1, height, width), lambda b: (count - 1 - b, 0, 0))
    return pl.BlockSpec((1, height, width), lambda b: (b, 0, 0))


def kernel_params():
    return pltpu.CompilerParams(dimension_semantics=("arbitrary",))


def attend_forward(queries, keys, values, decays):
    rows = queries.shape[0]
    block = block_of(rows)
    count = rows // block
    row_k = row_spec(block, HEAD_K, count, False)
    row_v = row_spec(block, HEAD_V, count, False)
    return pl.pallas_call(
        forward_kernel,
        grid=(count,),
        in_specs=[row_k, row_k, row_v, row_k],
        out_specs=[
            row_v,
            row_k,
            cube_spec(HEAD_V, HEAD_K, count, False),
            cube_spec(8, HEAD_K, count, False),
        ],
        out_shape=[
            jax.ShapeDtypeStruct((rows, HEAD_V), F32),
            jax.ShapeDtypeStruct((rows, HEAD_K), F32),
            jax.ShapeDtypeStruct((count, HEAD_V, HEAD_K), F32),
            jax.ShapeDtypeStruct((count, 8, HEAD_K), F32),
        ],
        scratch_shapes=[pltpu.VMEM((HEAD_V, HEAD_K), F32), pltpu.VMEM((8, HEAD_K), F32)],
        compiler_params=kernel_params(),
        name="recurrence_forward",
    )(queries, keys, values, decays)


def attend_state(keys, values, decays):
    rows = keys.shape[0]
    block = block_of(rows)
    count = rows // block
    row_k = row_spec(block, HEAD_K, count, False)
    row_v = row_spec(block, HEAD_V, count, False)
    return pl.pallas_call(
        state_kernel,
        grid=(count,),
        in_specs=[row_k, row_v, row_k],
        out_specs=pl.BlockSpec((HEAD_V, HEAD_K), lambda b: (0, 0)),
        out_shape=jax.ShapeDtypeStruct((HEAD_V, HEAD_K), F32),
        scratch_shapes=[pltpu.VMEM((HEAD_V, HEAD_K), F32)],
        compiler_params=kernel_params(),
        name="recurrence_state",
    )(keys, values, decays)


def attend_backward(queries, keys, values, decays, grads, states, before, entry, exit_grad):
    rows = queries.shape[0]
    block = block_of(rows)
    count = rows // block
    row_k = row_spec(block, HEAD_K, count, True)
    row_v = row_spec(block, HEAD_V, count, True)
    whole = pl.BlockSpec((HEAD_V, HEAD_K), lambda b: (0, 0))
    return pl.pallas_call(
        backward_kernel,
        grid=(count,),
        in_specs=[
            row_k,
            row_k,
            row_v,
            row_k,
            row_v,
            cube_spec(HEAD_V, HEAD_K, count, True),
            cube_spec(8, HEAD_K, count, True),
            whole,
            whole,
        ],
        out_specs=[row_k, row_k, row_v, row_k],
        out_shape=[
            jax.ShapeDtypeStruct((rows, HEAD_K), BF16),
            jax.ShapeDtypeStruct((rows, HEAD_K), BF16),
            jax.ShapeDtypeStruct((rows, HEAD_V), BF16),
            jax.ShapeDtypeStruct((rows, HEAD_K), F32),
        ],
        scratch_shapes=[pltpu.VMEM((HEAD_V, HEAD_K), F32)],
        compiler_params=kernel_params(),
        name="recurrence_backward",
    )(queries, keys, values, decays, grads, states, before, entry, exit_grad)


class Place:
    def __init__(self):
        self.rows = lax.axis_size("row")
        self.cols = lax.axis_size("col")
        self.groups = lax.axis_size("dp")
        self.row = lax.axis_index("row")
        self.col = lax.axis_index("col")
        self.group = lax.axis_index("dp")

    def from_row(self, x, step):
        n = self.rows
        return lax.ppermute(x, "row", [((i + step) % n, i) for i in range(n)])

    def to_row(self, x, step):
        n = self.rows
        return lax.ppermute(x, "row", [(i, (i + step) % n) for i in range(n)])

    def swap_group(self, x, bit):
        return lax.ppermute(x, "dp", [(i, i ^ bit) for i in range(self.groups)])

    def home_pairs(self, k):
        pairs = []
        for x in range(self.rows):
            for z in range(self.cols):
                slot = (x - k) % self.rows
                place = z * self.rows + slot
                pairs.append((x * self.cols + z, place))
        return pairs

    def to_home(self, x):
        high = x.shape[0] // self.rows
        wide = x.shape[1]
        out = jnp.zeros((high, wide * self.rows), x.dtype)
        own_slot = (self.row * self.cols + self.col) % self.rows
        for k in range(self.rows):
            slot = (self.row - k) % self.rows
            piece = lax.dynamic_slice_in_dim(x, slot * high, high, 0)
            piece = lax.ppermute(piece, ("row", "col"), self.home_pairs(k))
            at = (own_slot + k - self.row) % self.rows
            out = lax.dynamic_update_slice_in_dim(out, piece, at * wide, 1)
        return out

    def from_home(self, y):
        high = y.shape[0]
        wide = y.shape[1] // self.rows
        out = jnp.zeros((high * self.rows, wide), y.dtype)
        own_slot = (self.row * self.cols + self.col) % self.rows
        for k in range(self.rows):
            at = (own_slot + k - self.row) % self.rows
            piece = lax.dynamic_slice_in_dim(y, at * wide, wide, 1)
            pairs = [(home, first) for first, home in self.home_pairs(k)]
            piece = lax.ppermute(piece, ("row", "col"), pairs)
            slot = (self.row - k) % self.rows
            out = lax.dynamic_update_slice_in_dim(out, piece, slot * high, 0)
        return out

    def join(self, mine, other, bit):
        high = (self.group & bit) != 0
        return jnp.concatenate([jnp.where(high, other, mine), jnp.where(high, mine, other)], axis=0)

    def blocks_of(self, own):
        blocks = [own]
        high = own.shape[0] // self.groups
        share = lax.dynamic_slice_in_dim(own, self.group * high, high, 0)
        for step in range(1, self.rows):
            part = self.from_row(share, step)
            bit = 1
            while bit < self.groups:
                part = self.join(part, self.swap_group(part, bit), bit)
                bit *= 2
            blocks.append(part)
        return blocks

    def halves(self, x):
        wide = x.shape[1] // 2
        bit = self.group & 1
        keep = lax.dynamic_slice_in_dim(x, bit * wide, wide, 1)
        send = lax.dynamic_slice_in_dim(x, (1 - bit) * wide, wide, 1)
        return (keep, send)

    def reduce_weight(self, product):
        sent = [self.swap_group(part.astype(BF16), 1) for part in product("send")]
        kept = product("keep")
        summed = [a + b.astype(F32) for a, b in zip(kept, sent)]
        own = summed[0]
        for step in range(1, self.rows):
            own = own + self.to_row(summed[step].astype(BF16), step).astype(F32)
        bit = 2
        while bit < self.groups:
            high = own.shape[0] // 2
            side = jnp.where((self.group & bit) != 0, 1, 0)
            keep = lax.dynamic_slice_in_dim(own, side * high, high, 0)
            send = lax.dynamic_slice_in_dim(own, (1 - side) * high, high, 0)
            own = keep + self.swap_group(send.astype(BF16), bit).astype(F32)
            bit *= 2
        own = own.astype(BF16)
        bit //= 2
        while bit >= 1:
            own = self.join(own, self.swap_group(own, bit), bit)
            bit //= 2
        return own.astype(F32)


def gather_tokens(x):
    return lax.all_gather(x, "col", axis=0, tiled=True)


def scatter_tokens(parts):
    return lax.psum_scatter(
        jnp.concatenate([part.astype(BF16) for part in parts], axis=1),
        "col",
        scatter_dimension=0,
        tiled=True,
    ).astype(F32)


def columns(x, count):
    wide = x.shape[1] // count
    return [x[:, i * wide : (i + 1) * wide] for i in range(count)]


def over_features(parts, blocks):
    total = dot(parts[0], blocks[0], NN)
    for part, block in zip(parts[1:], blocks[1:]):
        total = total + dot(part, block, NN)
    return total


def over_features_back(parts, blocks):
    total = dot(parts[0], blocks[0], NT)
    for part, block in zip(parts[1:], blocks[1:]):
        total = total + dot(part, block, NT)
    return total


def norm_factor(values):
    return lax.rsqrt(jnp.mean(values * values, axis=1, keepdims=True) + EPSILON)


def norm_backward(values, factor, gains, upstream):
    weighted = upstream * gains
    inner = jnp.sum(weighted * values, axis=1, keepdims=True)
    grad_values = factor * weighted - values * (
        factor * factor * factor * inner / values.shape[1]
    )
    return (grad_values, jnp.sum(upstream * values * factor, axis=0))


def body(
    hidden_in,
    seq_lengths,
    gain_attn,
    w_query,
    w_key,
    w_value,
    w_outgate,
    rank_down,
    rank_up,
    decay_bias,
    gain_head,
    w_output,
    gain_ffn,
    w_gate,
    w_up,
    w_down,
    cotangent,
):
    place = Place()
    rows, cols = place.rows, place.cols
    half_rows = SLOT // rows
    home_rows = half_rows // cols
    wide = hidden_in.shape[1]
    rank = rank_down.shape[1]
    head_wide = gain_head.shape[0]

    residual_in = place.to_home(hidden_in).astype(F32)
    w_in = jnp.concatenate([w_query, w_key, w_value, w_outgate], axis=1)
    w_two = jnp.concatenate([w_gate, w_up], axis=1)
    in_blocks = place.blocks_of(w_in)
    small = jnp.concatenate([gain_attn, gain_ffn, gain_head, rank_down.reshape(-1)])
    smalls = [small] + [place.from_row(small, step) for step in range(1, rows)]
    gain_one = jnp.concatenate([s[:wide] for s in smalls]).astype(F32)
    gain_two = jnp.concatenate([s[wide : 2 * wide] for s in smalls]).astype(F32)
    heads = jnp.stack([s[2 * wide : 2 * wide + head_wide] for s in smalls])
    gain_mix = jnp.roll(heads, place.row, axis=0).reshape(-1).astype(F32)
    down_blocks = [s[2 * wide + head_wide :].reshape(wide, rank) for s in smalls]

    place_home = place.row * half_rows + place.col * home_rows
    valid = (place_home + jnp.arange(home_rows) < seq_lengths[0]).astype(F32)[:, None]

    factor_one = norm_factor(residual_in)
    normed_one = (residual_in * factor_one * gain_one).astype(BF16)
    tokens_one = gather_tokens(normed_one)
    ones = columns(tokens_one, rows)
    pre = over_features(ones, in_blocks)
    queries = pre[:, :HEAD_K].astype(BF16)
    keys = pre[:, HEAD_K : 2 * HEAD_K].astype(BF16)
    values = pre[:, 2 * HEAD_K : 2 * HEAD_K + HEAD_V].astype(BF16)
    outgate = pre[:, 2 * HEAD_K + HEAD_V :]
    rank_mid = over_features(ones, down_blocks).astype(BF16)
    decay_logits = dot(rank_mid, rank_up, NN) + decay_bias
    decays = jax.nn.log_sigmoid(decay_logits) / 16.0

    ending = attend_state(keys, values, decays)
    steps = [(i, i + 1) for i in range(rows - 1)]
    entry = lax.ppermute(ending, "row", steps)
    if rows > 2:
        all_fade = jnp.exp(jnp.sum(decays, axis=0))[None, :]
        for _ in range(rows - 2):
            entry = lax.ppermute(entry * all_fade + ending, "row", steps)
    mixed, faded, states, before = attend_forward(queries, keys, values, decays)
    mixed = mixed + dot(faded, entry, NT, HIGH)
    factor_head = norm_factor(mixed)
    normed_head = mixed * factor_head * gain_mix
    out_sig = jax.nn.sigmoid(outgate)
    out_act = outgate * out_sig
    gated = (normed_head * out_act).astype(BF16)
    out_blocks = place.blocks_of(w_output)
    attn_out = scatter_tokens([dot(gated, block, NN) for block in out_blocks])
    residual_mid = residual_in + attn_out

    factor_two = norm_factor(residual_mid)
    normed_two = (residual_mid * factor_two * gain_two).astype(BF16)
    tokens_two = gather_tokens(normed_two)
    twos = columns(tokens_two, rows)
    two_blocks = place.blocks_of(w_two)
    both = over_features(twos, two_blocks)
    hidden_wide = w_gate.shape[1]
    gate_pre = both[:, :hidden_wide]
    up_pre = both[:, hidden_wide:]
    swish_sig = jax.nn.sigmoid(gate_pre)
    swish_out = gate_pre * swish_sig
    hidden = (swish_out * up_pre).astype(BF16)
    ffn_blocks = place.blocks_of(w_down)

    upstream = valid * place.to_home(cotangent).astype(F32)
    ffn_grad = gather_tokens(upstream.astype(BF16))
    ffn_grads = columns(ffn_grad, rows)
    hidden_grad = over_features_back(ffn_grads, ffn_blocks)
    swish_slope = swish_sig * (1.0 + gate_pre * (1.0 - swish_sig))
    gate_grad = (hidden_grad * up_pre * swish_slope).astype(BF16)
    up_grad = (hidden_grad * swish_out).astype(BF16)
    both_grad = jnp.concatenate([gate_grad, up_grad], axis=1)

    normed_two_grad = scatter_tokens([dot(both_grad, block, NT) for block in two_blocks])
    mid_part, gain_two_grad = norm_backward(residual_mid, factor_two, gain_two, normed_two_grad)
    mid_grad = upstream + mid_part
    ffn_out = scatter_tokens([dot(hidden, block, NN) for block in ffn_blocks])
    block_out = place.from_home((valid * (residual_mid + ffn_out)).astype(BF16))

    attn_grad = gather_tokens(mid_grad.astype(BF16))
    attn_grads = columns(attn_grad, rows)
    gated_grad = over_features_back(attn_grads, out_blocks)
    head_grad = gated_grad * out_act
    out_slope = out_sig * (1.0 + outgate * (1.0 - out_sig))
    outgate_grad = (gated_grad * normed_head * out_slope).astype(BF16)
    mixed_grad, gain_mix_grad = norm_backward(mixed, factor_head, gain_mix, head_grad)

    start_grad = dot(mixed_grad, faded, TN, HIGH)
    back = [(i + 1, i) for i in range(rows - 1)]
    exit_grad = lax.ppermute(start_grad, "row", back)
    if rows > 2:
        for _ in range(rows - 2):
            exit_grad = lax.ppermute(exit_grad * all_fade + start_grad, "row", back)
    query_grad, key_grad, value_grad, decay_grad = attend_backward(
        queries, keys, values, decays, mixed_grad, states, before, entry, exit_grad
    )
    logit_grad = decay_grad * jax.nn.sigmoid(-decay_logits) / 16.0
    rank_up_part = dot(rank_mid.astype(F32), logit_grad, TN, HIGHEST)
    bias_part = jnp.sum(logit_grad, axis=0)
    rank_term = dot(logit_grad, rank_up.astype(F32), NT, HIGHEST)
    rank_grad = lax.psum(rank_term, "col").astype(BF16)
    in_grad = jnp.concatenate([query_grad, key_grad, value_grad, outgate_grad], axis=1)
    normed_one_grad = scatter_tokens([dot(in_grad, block, NT) for block in in_blocks])
    own_rank = lax.dynamic_slice_in_dim(rank_grad, place.col * home_rows, home_rows, 0)
    normed_one_grad = normed_one_grad + jnp.concatenate(
        [dot(own_rank, block, NT) for block in down_blocks], axis=1
    )
    input_part, gain_one_grad = norm_backward(residual_in, factor_one, gain_one, normed_one_grad)
    grad_input = place.from_home((mid_grad + input_part).astype(BF16)).astype(F32)

    def tall(tokens, grads):
        def product(which):
            pick = 0 if which == "keep" else 1
            return [dot(place.halves(x)[pick], grads, TN) for x in columns(tokens, rows)]

        return place.reduce_weight(product)

    def broad(left, grads):
        def product(which):
            pick = 0 if which == "keep" else 1
            return columns(dot(place.halves(left)[pick], grads, TN), rows)

        return place.reduce_weight(product)

    grad_down = broad(hidden, ffn_grad)
    grad_two = tall(tokens_two, both_grad)
    grad_output = broad(gated, attn_grad)
    grad_in = tall(tokens_one, in_grad)

    def absolute(x):
        return jnp.roll(x.reshape((rows, -1) + x.shape[1:]), place.row, axis=0).reshape(x.shape)

    down_part = jnp.concatenate([dot(x, rank_grad, TN) for x in ones], axis=0)
    decay_all = lax.psum(
        (rank_up_part, bias_part, absolute(down_part)), ("dp", "row")
    )
    gains_all = lax.psum(
        (absolute(gain_one_grad), gain_mix_grad, absolute(gain_two_grad)), ("dp", "row", "col")
    )

    def mine(x):
        size = x.shape[0] // rows
        return lax.dynamic_slice_in_dim(x, place.row * size, size, 0)

    return (
        block_out,
        grad_input,
        mine(gains_all[0]),
        grad_in[:, :HEAD_K],
        grad_in[:, HEAD_K : 2 * HEAD_K],
        grad_in[:, 2 * HEAD_K : 2 * HEAD_K + HEAD_V],
        grad_in[:, 2 * HEAD_K + HEAD_V :],
        mine(decay_all[2]),
        decay_all[0],
        decay_all[1],
        mine(gains_all[1]),
        grad_output,
        mine(gains_all[2]),
        grad_two[:, :hidden_wide],
        grad_two[:, hidden_wide:],
        grad_down,
    )


def solution(mesh):
    placed = (
        P(("dp", "col"), "row"),
        P("dp"),
        P("row"),
        P("row", "col"),
        P("row", "col"),
        P("row", "col"),
        P("row", "col"),
        P("row", None),
        P(None, "col"),
        P("col"),
        P("row"),
        P("col", "row"),
        P("row"),
        P("row", "col"),
        P("row", "col"),
        P("col", "row"),
        P(("dp", "col"), "row"),
    )
    return jax.shard_map(
        body,
        mesh=mesh,
        in_specs=placed,
        out_specs=(
            P(("dp", "col"), "row"),
            P(("dp", "col"), "row"),
            P("row"),
            P("row", "col"),
            P("row", "col"),
            P("row", "col"),
            P("row", "col"),
            P("row", None),
            P(None, "col"),
            P("col"),
            P("row"),
            P("col", "row"),
            P("row"),
            P("row", "col"),
            P("row", "col"),
            P("col", "row"),
        ),
        check_vma=False,
    )
```

time: 2080 us -> 1030 us (0.50)
  waiting for transfers between devices: 1220 us -> 439 us
  blocking collectives: 326 us -> 134 us
  matrix products: 222 us -> 133 us
  starting transfers between devices: 2.54 us -> 55.5 us
  Pallas kernels: 0 us -> 48.2 us
  local copies, waits for them, and re-layouts: 126 us -> 82.1 us
  other arithmetic: 154 us -> 114 us
    reduce_scatter x12 -> x4, waiting for transfers between devices: 683 us -> 50.5 us  [scatter_tokens(): lax.psum_scatter(jnp.concatenate([part.astype(BF16) for part in parts], a...]
    ppermute x0 -> x47, waiting for transfers between devices: none -> 347 us  [the longest x28 229 us: swap_group(): return lax.ppermute(x, 'dp', [(i, i ^ bit) for i in range(self.groups)])]
    all_gather x12 -> x4, waiting for transfers between devices: 382 us -> 41.3 us  [gather_tokens(): return lax.all_gather(x, 'col', axis=0, tiled=True)]
    psum x12 -> x3, blocking collectives: 326 us -> 134 us  [the longest x1 63.1 us: body(): lax.psum((absolute(gain_one_grad), gain_mix_grad, absolute(gain_two_grad)...]
    psum x1, waiting for transfers between devices: 153 us -> 0.01 us  [body(): lax.psum((rank_up_part, bias_part, absolute(down_part)), ('dp', 'row'))]
    dot_general x42 -> x39, matrix products: 222 us -> 133 us  [dot(): lax.dot_general(left, right, dims, precision=precision, preferred_element...]
    dynamic_slice x81 -> x12, local copies, waits for them, and re-layouts: 91.5 us -> 14 us  [the longest x4 5.23 us: blocks_of(): share = lax.dynamic_slice_in_dim(own, self.group * high, high, 0)]
    ppermute x0 -> x47, starting transfers between devices: none -> 54.8 us  [the longest x28 18.1 us: swap_group(): return lax.ppermute(x, 'dp', [(i, i ^ bit) for i in range(self.groups)])]
  transfers between devices with their start and end apart: 25 -> 56, of which waited for: 21 -> 21; matrix products, arithmetic and copies ran while one was open for 17% -> 24% of each run, Pallas kernels for 0% -> 5%
where the time goes in v1:
time: 1030 us; the launch traced here: 1020 us
  waiting for transfers between devices  439 us (43%)
  blocking collectives  134 us (13%)
  matrix products  133 us (13%)
  other arithmetic  114 us (11%)
  local copies, waits for them, and re-layouts  82.1 us (8%)
  starting transfers between devices  55.5 us (5%)
  Pallas kernels  48.2 us (5%)
  between operations  16.7 us (2%)
    ppermute x28, waiting for transfers between devices, swap_group(): return lax.ppermute(x, 'dp', [(i, i ^ bit) for i in range(self.groups)])  229 us
    dot_general x39, matrix products, dot(): lax.dot_general(left, right, dims, precision=precision, preferred_element...  133 us
    psum x1, blocking collectives, body(): lax.psum((absolute(gain_one_grad), gain_mix_grad, absolute(gain_two_grad)...  63.1 us
    psum x1, blocking collectives, body(): lax.psum((rank_up_part, bias_part, absolute(down_part)), ('dp', 'row'))  53.4 us
    reduce_scatter x4, waiting for transfers between devices, scatter_tokens(): lax.psum_scatter(jnp.concatenate([part.astype(BF16) for part in parts], a...  50.5 us
    ppermute x5, waiting for transfers between devices, from_row(): return lax.ppermute(x, 'row', [((i + step) % n, i) for i in range(n)])  46.6 us
    all_gather x4, waiting for transfers between devices, gather_tokens(): return lax.all_gather(x, 'col', axis=0, tiled=True)  41.3 us
    ppermute x4, waiting for transfers between devices, to_home(): piece = lax.ppermute(piece, ('row', 'col'), self.home_pairs(k))  39 us
  transfers between devices with their start and end apart: 56, of which 21 were waited for; matrix products, arithmetic and copies ran while one was open for 24% of the time, Pallas kernels for 5%

profile of v1, /device:TPU:10, one launch (start us, length us, event | category | flops | bytes accessed | tf_op | source)
XLA Modules:
  0.0 1023.0 jit_solution(8610256769317114181)
XLA Ops:
  25.6 23.8 %collective-permute-done.2 = bf16[18688]{0:T(1024)(128)(2,1)S(1)} collective-permute-done((bf16[18688]{0:T(1024)(128)(2,1)S(1)}, bf16[18688]{0:T(1024)(128)(2,1)S(1)}, u32[]{:S(2)}, u32[]{:S(2)}) %collective-permute-start.2) | collective-permute-done | bytes 37408 | tf_op jit(solution)/shard_map/ppermute | solution.py:276
  71.3 36.4 %collective-permute-done.5 = bf16[512,2048]{1,0:T(8,128)(2,1)} collective-permute-done((bf16[512,2048]{1,0:T(8,128)(2,1)}, bf16[512,2048]{1,0:T(8,128)(2,1)}, u32[]{:S(2)}, u32[]{:S(2)}) %collective-permute-start.5) | collective-permute-done | bytes 2097184 | tf_op jit(solution)/shard_map/ppermute | solution.py:283
  107.7 5.6 broadcast_select_fusion.7
  129.2 9.9 recurrence_state.1
  144.9 11.9 %collective-permute-done.9 = bf16[256,1024]{1,0:T(8,128)(2,1)} collective-permute-done((bf16[256,1024]{1,0:T(8,128)(2,1)}, bf16[256,1024]{1,0:T(8,128)(2,1)}, u32[]{:S(2)}, u32[]{:S(2)}) %collective-permute-start.9) | collective-permute-done | bytes 524320 | tf_op jit(solution)/shard_map/ppermute | solution.py:283
  159.2 15.6 %recurrence_forward.1 = (f32[640,512]{1,0:T(8,128)}, f32[640,512]{1,0:T(8,128)}, f32[10,512,512]{2,1,0:T(8,128)}, f32[10,8,512]{2,1,0:T(8,128)}) custom-call(bf16[640,512]{1,0:T(8,128)(2,1)} %get-tuple-element.80.q_ref, bf16[640,512]{1,0:T(8,128)(2,1)} %get-tuple-element.79.k_ref, bf16[640,512]{1,0:T(8,128)(2,1)} %get-tuple-element.78.v_ref, ...), custom_call_target="tpu_custom_call" | custom-call | tf_op jit(solution)/shard_map/recurrence_forward/pallas_call | solution.py:191
  186.6 5.7 collective-permute-start.18
  201.1 13.0 %collective-permute-done.18 = bf16[160,1024]{1,0:T(8,128)(2,1)} collective-permute-done((bf16[160,1024]{1,0:T(8,128)(2,1)}, bf16[160,1024]{1,0:T(8,128)(2,1)}, u32[]{:S(2)}, u32[]{:S(2)}) %collective-permute-start.18) | collective-permute-done | bytes 327712 | tf_op jit(solution)/shard_map/ppermute | solution.py:302
  215.2 26.0 %collective-permute-done.19 = bf16[160,1024]{1,0:T(8,128)(2,1)} collective-permute-done((bf16[160,1024]{1,0:T(8,128)(2,1)}, bf16[160,1024]{1,0:T(8,128)(2,1)}, u32[]{:S(2)}, u32[]{:S(2)}) %collective-permute-start.19) | collective-permute-done | bytes 327712 | tf_op jit(solution)/shard_map/ppermute | solution.py:302
  245.1 17.9 %collective-permute-done.13 = bf16[352,1024]{1,0:T(8,128)(2,1)} collective-permute-done((bf16[352,1024]{1,0:T(8,128)(2,1)S(1)}, bf16[352,1024]{1,0:T(8,128)(2,1)}, u32[]{:S(2)}, u32[]{:S(2)}) %collective-permute-start.13) | collective-permute-done | bytes 720928 | tf_op jit(solution)/shard_map/ppermute | solution.py:276
  278.5 92.3 %collective-permute-done.15 = bf16[704,1024]{1,0:T(8,128)(2,1)S(1)} collective-permute-done((bf16[704,1024]{1,0:T(8,128)(2,1)S(1)}, bf16[704,1024]{1,0:T(8,128)(2,1)S(1)}, u32[]{:S(2)}, u32[]{:S(2)}) %collective-permute-start.15) | collective-permute-done | bytes 1441824 | tf_op jit(solution)/shard_map/ppermute | solution.py:283
  383.7 9.9 fusion.97
  393.7 8.5 convolution_add_fusion
  402.2 8.0 multiply_convert_fusion.1
  410.2 6.1 fusion.8
  422.3 50.5 %reduce-scatter.9.cloned.1.call-done = bf16[160,2048]{1,0:T(8,128)(2,1)} async-done(((bf16[640,2048]{1,0:T(8,128)(2,1)}), bf16[160,2048]{1,0:T(8,128)(2,1)}) %reduce-scatter.9.cloned.1.call-update) | async-done | bytes 655376 | tf_op jit(solution)/shard_map/reduce_scatter | solution.py:373
  491.7 41.3 %all-gather.11.cloned.1.call-done = bf16[640,2048]{1,0:T(8,128)(2,1)} async-done(((bf16[160,2048]{1,0:T(8,128)(2,1)}), bf16[640,2048]{1,0:T(8,128)(2,1)}) %all-gather.11.cloned.1.call-update) | async-done | bytes 2621456 | tf_op jit(solution)/shard_map/all_gather | solution.py:369
  560.4 10.8 %collective-permute-done.20.exit_ref = f32[512,512]{1,0:T(8,128)} collective-permute-done((f32[512,512]{1,0:T(8,128)S(1)}, f32[512,512]{1,0:T(8,128)}, u32[]{:S(2)}, u32[]{:S(2)}) %collective-permute-start.20) | collective-permute-done | bytes 1048608 | tf_op jit(solution)/shard_map/ppermute | solution.py:525
  571.2 22.7 %recurrence_backward.1 = (bf16[640,512]{1,0:T(8,128)(2,1)}, bf16[640,512]{1,0:T(8,128)(2,1)}, bf16[640,512]{1,0:T(8,128)(2,1)}, f32[640,512]{1,0:T(8,128)}) custom-call(bf16[640,512]{1,0:T(8,128)(2,1)} %get-tuple-element.80.q_ref, bf16[640,512]{1,0:T(8,128)(2,1)} %get-tuple-element.79.k_ref, bf16[640,512]{1,0:T(8,128)(2,1)} %get-tuple-element.78.v_ref, ...), custom_call_target="tpu_custom_call" | custom-call | tf_op jit(solution)/shard_map/recurrence_backward/pallas_call | solution.py:238
  599.0 17.7 %psum.49 = bf16[640,16]{0,1:T(8,128)(2,1)} all-reduce(f32[640,16]{0,1:T(8,128)} %fusion.124), channel_id=1, replica_groups=mesh['dp'=4,'row'=2,'col'=4] {'col'}, use_global_device_ids=true, to_apply=%region_9.10 | all-reduce | flops 10240 | bytes 61440 | tf_op jit(solution)/shard_map/psum | solution.py:536
  624.3 6.0 convolution_convert_fusion.6
  635.2 7.2 add_convert_fusion
  655.9 10.4 %collective-permute-done.44 = bf16[352,1024]{1,0:T(8,128)(2,1)} collective-permute-done((bf16[352,1024]{1,0:T(8,128)(2,1)}, bf16[352,1024]{1,0:T(8,128)(2,1)}, u32[]{:S(2)}, u32[]{:S(2)}) %collective-permute-start.44) | collective-permute-done | bytes 720928 | tf_op jit(solution)/shard_map/ppermute | solution.py:283
  681.1 21.6 %collective-permute-done.37 = bf16[512,2816]{1,0:T(8,128)(2,1)} collective-permute-done((bf16[512,2816]{1,0:T(8,128)(2,1)}, bf16[512,2816]{1,0:T(8,128)(2,1)}, u32[]{:S(2)}, u32[]{:S(2)}) %collective-permute-start.37) | collective-permute-done | bytes 2883616 | tf_op jit(solution)/shard_map/ppermute | solution.py:280
  723.0 14.6 %collective-permute-done.38 = bf16[256,2816]{1,0:T(8,128)(2,1)} collective-permute-done((bf16[256,2816]{1,0:T(8,128)(2,1)}, bf16[256,2816]{1,0:T(8,128)(2,1)}, u32[]{:S(2)}, u32[]{:S(2)}) %collective-permute-start.38) | collective-permute-done | bytes 1441824 | tf_op jit(solution)/shard_map/ppermute | solution.py:283
  748.6 16.9 %collective-permute-done.39 = bf16[256,2816]{1,0:T(8,128)(2,1)S(1)} collective-permute-done((bf16[256,2816]{1,0:T(8,128)(2,1)S(1)}, bf16[256,2816]{1,0:T(8,128)(2,1)S(1)}, u32[]{:S(2)}, u32[]{:S(2)}) %collective-permute-start.39) | collective-permute-done | bytes 1441824 | tf_op jit(solution)/shard_map/ppermute | solution.py:283
  789.8 53.4 %all-reduce.1 = (f32[16,512]{1,0:T(8,128)}, f32[512]{0:T(512)}) all-reduce(f32[16,512]{1,0:T(8,128)} %fusion.125, f32[512]{0:T(512)S(1)} %copy-done.89), channel_id=1, replica_groups=mesh['dp'=4,'row'=2,'col'=4] {'dp','row'}, use_global_device_ids=true, to_apply=%region_14.16 | all-reduce | flops 8704 | bytes 69632 | tf_op jit(solution)/shard_map/psum | solution.py:569
  843.2 5.7 fusion.54
  861.1 20.3 %collective-permute-done.26 = bf16[256,2048]{1,0:T(8,128)(2,1)S(1)} collective-permute-done((bf16[256,2048]{1,0:T(8,128)(2,1)S(1)}, bf16[256,2048]{1,0:T(8,128)(2,1)S(1)}, u32[]{:S(2)}, u32[]{:S(2)}) %collective-permute-start.26) | collective-permute-done | bytes 1048608 | tf_op jit(solution)/shard_map/ppermute | solution.py:283
  892.5 15.3 %collective-permute-done.27 = bf16[256,2048]{1,0:T(8,128)(2,1)} collective-permute-done((bf16[256,2048]{1,0:T(8,128)(2,1)}, bf16[256,2048]{1,0:T(8,128)(2,1)}, u32[]{:S(2)}, u32[]{:S(2)}) %collective-permute-start.27) | collective-permute-done | bytes 1048608 | tf_op jit(solution)/shard_map/ppermute | solution.py:283
  921.5 9.5 fusion.114
  937.9 63.1 %all-reduce = (f32[2048]{0:T(1024)S(1)}, f32[512]{0:T(512)S(1)}, f32[2048]{0:T(1024)S(1)}) all-reduce(f32[2048]{0:T(1024)S(1)} %bitcast.60, f32[512]{0:T(512)S(1)} %copy-done.92, f32[2048]{0:T(1024)S(1)} %bitcast.59), channel_id=1, replica_groups=mesh['dp'=4,'row'=2,'col'=4] {'dp','row','col'}, use_global_device_ids=true, to_apply=%region_12.14 | all-reduce | flops 4608 | bytes 36864 | tf_op jit(solution)/shard_map/psum | solution.py:572
  (493 shorter events, 328.7 us)
Async XLA Ops:
  7.2 106.1 %all-gather.5.cloned.1.call-start = ((), (), s32[]{:S(2)}) async-start(), calls=%async_computation.4 | async-start | bytes 3276800 | tf_op jit(solution)/shard_map/all_gather | solution.py:369
  16.5 35.9 %collective-permute-start.3 = (bf16[256,2048]{1,0:T(8,128)(2,1)}, bf16[256,2048]{1,0:T(8,128)(2,1)}, u32[]{:S(2)}, u32[]{:S(2)}) collective-permute-start(bf16[256,2048]{1,0:T(8,128)(2,1)} %constant_dynamic-slice_fusion.15), channel_id=1, source_target_pairs={{4,0},{0,4},{5,1},{1,5},{6,2},{2,6},{7,3},{3,7},{12,8},{8,12},{13,... | collective-permute-start | bytes 3145736 | tf_op jit(solution)/shard_map/ppermute | solution.py:276
  54.6 212.0 %reduce-scatter.5.cloned.1.call-start = ((), (), s32[]{:S(2)}) async-start(), calls=%async_computation.5 | async-start | bytes 3276800 | tf_op jit(solution)/shard_map/reduce_scatter | solution.py:373
  59.7 48.0 %collective-permute-start.5 = (bf16[512,2048]{1,0:T(8,128)(2,1)}, bf16[512,2048]{1,0:T(8,128)(2,1)}, u32[]{:S(2)}, u32[]{:S(2)}) collective-permute-start(bf16[512,2048]{1,0:T(8,128)(2,1)} %pad_maximum_fusion.15), channel_id=1, source_target_pairs={{0,16},{8,24},{16,0},{24,8},{1,17},{9,25},{17,1},{25,9},{2,18},{10... | collective-permute-start | bytes 6291464 | tf_op jit(solution)/shard_map/ppermute | solution.py:283
  71.3 69.4 %collective-permute-start.8 = (bf16[128,1024]{1,0:T(8,128)(2,1)}, bf16[128,1024]{1,0:T(8,128)(2,1)}, u32[]{:S(2)}, u32[]{:S(2)}) collective-permute-start(bf16[128,1024]{1,0:T(8,128)(2,1)} %collective-permute-done.7), channel_id=1, source_target_pairs={{0,8},{8,0},{16,24},{24,16},{1,9},{9,1},{17,25},{25,17},{2,10},{10... | collective-permute-start | bytes 786440 | tf_op jit(solution)/shard_map/ppermute | solution.py:283
  184.6 188.7 %all-gather.9.cloned.1.call-start = ((), (), s32[]{:S(2)}) async-start(), calls=%async_computation.8 | async-start | bytes 3276800 | tf_op jit(solution)/shard_map/all_gather | solution.py:369
  192.2 48.9 %collective-permute-start.19 = (bf16[160,1024]{1,0:T(8,128)(2,1)}, bf16[160,1024]{1,0:T(8,128)(2,1)}, u32[]{:S(2)}, u32[]{:S(2)}) collective-permute-start(bf16[160,1024]{1,0:T(8,128)(2,1)} %get-tuple-element.99), channel_id=1, source_target_pairs={{0,1},{1,3},{2,5},{3,7},{4,0},{5,2},{6,4},{7,6},{8,9},{9,11},{10,1... | collective-permute-start | bytes 983048 | tf_op jit(solution)/shard_map/ppermute | solution.py:302
  199.7 44.4 %collective-permute-start.10 = (bf16[256,2816]{1,0:T(8,128)(2,1)}, bf16[256,2816]{1,0:T(8,128)(2,1)}, u32[]{:S(2)}, u32[]{:S(2)}) collective-permute-start(bf16[256,2816]{1,0:T(8,128)(2,1)} %constant_dynamic-slice_fusion.12), channel_id=1, source_target_pairs={{4,0},{0,4},{5,1},{1,5},{6,2},{2,6},{7,3},{3,7},{12,8},{8,12},{13,... | collective-permute-start | bytes 4325384 | tf_op jit(solution)/shard_map/ppermute | solution.py:276
  244.1 139.6 %all-gather.7.cloned.1.call-start = ((), (), s32[]{:S(2)}) async-start(), calls=%async_computation.6 | async-start | bytes 3276800 | tf_op jit(solution)/shard_map/all_gather | solution.py:369
  271.3 201.5 %reduce-scatter.9.cloned.1.call-start = ((), (), s32[]{:S(2)}) async-start(), calls=%async_computation.9 | async-start | bytes 3276800 | tf_op jit(solution)/shard_map/reduce_scatter | solution.py:373
  274.9 103.9 %collective-permute-start.12 = (bf16[512,2816]{1,0:T(8,128)(2,1)}, bf16[512,2816]{1,0:T(8,128)(2,1)}, u32[]{:S(2)}, u32[]{:S(2)}) collective-permute-start(bf16[512,2816]{1,0:T(8,128)(2,1)} %pad_maximum_fusion.5), channel_id=1, source_target_pairs={{0,16},{8,24},{16,0},{24,8},{1,17},{9,25},{17,1},{25,9},{2,18},{10... | collective-permute-start | bytes 8650760 | tf_op jit(solution)/shard_map/ppermute | solution.py:283
  278.0 92.8 %collective-permute-start.15 = (bf16[704,1024]{1,0:T(8,128)(2,1)S(1)}, bf16[704,1024]{1,0:T(8,128)(2,1)S(1)}, u32[]{:S(2)}, u32[]{:S(2)}) collective-permute-start(bf16[704,1024]{1,0:T(8,128)(2,1)S(1)} %pad_maximum_fusion.25), channel_id=1, source_target_pairs={{0,16},{8,24},{16,0},{24,8},{1,17},{9,25},{17,1},{25,9},{2,18},{10... | collective-permute-start | bytes 4325384 | tf_op jit(solution)/shard_map/ppermute | solution.py:283
  422.0 110.9 %all-gather.11.cloned.1.call-start = ((), (), s32[]{:S(2)}) async-start(), calls=%async_computation.10 | async-start | bytes 3276800 | tf_op jit(solution)/shard_map/all_gather | solution.py:369
  479.3 369.6 %all-reduce.4.cloned.1.call-start = ((), (), s32[]{:S(2)}) async-start(), calls=%async_computation.12 | async-start | bytes 262144 | tf_op jit(solution)/shard_map/psum | solution.py:569
  486.7 148.6 %collective-permute-start.36 = (bf16[512,2816]{1,0:T(8,128)(2,1)}, bf16[512,2816]{1,0:T(8,128)(2,1)}, u32[]{:S(2)}, u32[]{:S(2)}) collective-permute-start(bf16[512,2816]{1,0:T(8,128)(2,1)} %convolution_convert_fusion), channel_id=1, source_target_pairs={{0,8},{8,0},{16,24},{24,16},{1,9},{9,1},{17,25},{25,17},{2,10},{10... | collective-permute-start | bytes 8650760 | tf_op jit(solution)/shard_map/ppermute | solution.py:283
  491.2 65.1 %collective-permute-start.42 = (bf16[704,1024]{1,0:T(8,128)(2,1)}, bf16[704,1024]{1,0:T(8,128)(2,1)}, u32[]{:S(2)}, u32[]{:S(2)}) collective-permute-start(bf16[704,1024]{1,0:T(8,128)(2,1)} %get-tuple-element.67), channel_id=1, source_target_pairs={{0,8},{8,0},{16,24},{24,16},{1,9},{9,1},{17,25},{25,17},{2,10},{10... | collective-permute-start | bytes 4325384 | tf_op jit(solution)/shard_map/ppermute | solution.py:283
  553.1 127.8 %collective-permute-start.35 = (bf16[512,2816]{1,0:T(8,128)(2,1)}, bf16[512,2816]{1,0:T(8,128)(2,1)}, u32[]{:S(2)}, u32[]{:S(2)}) collective-permute-start(bf16[512,2816]{1,0:T(8,128)(2,1)} %convolution_convert_fusion.1), channel_id=1, source_target_pairs={{0,8},{8,0},{16,24},{24,16},{1,9},{9,1},{17,25},{25,17},{2,10},{10... | collective-permute-start | bytes 8650760 | tf_op jit(solution)/shard_map/ppermute | solution.py:283
  553.1 91.9 %collective-permute-start.41 = (bf16[704,1024]{1,0:T(8,128)(2,1)}, bf16[704,1024]{1,0:T(8,128)(2,1)}, u32[]{:S(2)}, u32[]{:S(2)}) collective-permute-start(bf16[704,1024]{1,0:T(8,128)(2,1)} %get-tuple-element.66), channel_id=1, source_target_pairs={{0,8},{8,0},{16,24},{24,16},{1,9},{9,1},{17,25},{25,17},{2,10},{10... | collective-permute-start | bytes 4325384 | tf_op jit(solution)/shard_map/ppermute | solution.py:283
  560.4 84.6 %collective-permute-start.43 = (bf16[704,1024]{1,0:T(8,128)(2,1)}, bf16[704,1024]{1,0:T(8,128)(2,1)}, u32[]{:S(2)}, u32[]{:S(2)}) collective-permute-start(bf16[704,1024]{1,0:T(8,128)(2,1)} %fusion.2), channel_id=1, source_target_pairs={{0,4},{4,0},{1,5},{5,1},{2,6},{6,2},{3,7},{7,3},{8,12},{12,8},{9,1... | collective-permute-start | bytes 4325384 | tf_op jit(solution)/shard_map/ppermute | solution.py:280
  624.2 265.2 %reduce-scatter.11.cloned.1.call-start = ((), (), s32[]{:S(2)}) async-start(), calls=%async_computation.11 | async-start | bytes 3276800 | tf_op jit(solution)/shard_map/reduce_scatter | solution.py:373
  635.0 277.0 %reduce-scatter.7.cloned.1.call-start = ((), (), s32[]{:S(2)}) async-start(), calls=%async_computation.7 | async-start | bytes 3276800 | tf_op jit(solution)/shard_map/reduce_scatter | solution.py:373
  642.4 60.3 %collective-permute-start.37 = (bf16[512,2816]{1,0:T(8,128)(2,1)}, bf16[512,2816]{1,0:T(8,128)(2,1)}, u32[]{:S(2)}, u32[]{:S(2)}) collective-permute-start(bf16[512,2816]{1,0:T(8,128)(2,1)} %add_convert_fusion), channel_id=1, source_target_pairs={{0,4},{4,0},{1,5},{5,1},{2,6},{6,2},{3,7},{7,3},{8,12},{12,8},{9,1... | collective-permute-start | bytes 8650760 | tf_op jit(solution)/shard_map/ppermute | solution.py:280
  681.0 36.1 %collective-permute-start.46 = (bf16[704,1024]{1,0:T(8,128)(2,1)}, bf16[704,1024]{1,0:T(8,128)(2,1)}, u32[]{:S(2)}, u32[]{:S(2)}) collective-permute-start(bf16[704,1024]{1,0:T(8,128)(2,1)} %pad_maximum_fusion.26), channel_id=1, source_target_pairs={{0,8},{8,0},{16,24},{24,16},{1,9},{9,1},{17,25},{25,17},{2,10},{10... | collective-permute-start | bytes 4325384 | tf_op jit(solution)/shard_map/ppermute | solution.py:283
  769.4 82.4 %collective-permute-start.23 = (bf16[512,2048]{1,0:T(8,128)(2,1)}, bf16[512,2048]{1,0:T(8,128)(2,1)}, u32[]{:S(2)}, u32[]{:S(2)}) collective-permute-start(bf16[512,2048]{1,0:T(8,128)(2,1)} %convolution_convert_fusion.4), channel_id=1, source_target_pairs={{0,8},{8,0},{16,24},{24,16},{1,9},{9,1},{17,25},{25,17},{2,10},{10... | collective-permute-start | bytes 6291464 | tf_op jit(solution)/shard_map/ppermute | solution.py:283
  774.9 76.9 %collective-permute-start.25 = (bf16[512,2048]{1,0:T(8,128)(2,1)}, bf16[512,2048]{1,0:T(8,128)(2,1)}, u32[]{:S(2)}, u32[]{:S(2)}) collective-permute-start(bf16[512,2048]{1,0:T(8,128)(2,1)} %add_convert_fusion.1), channel_id=1, source_target_pairs={{0,4},{4,0},{1,5},{5,1},{2,6},{6,2},{3,7},{7,3},{8,12},{12,8},{9,1... | collective-permute-start | bytes 6291464 | tf_op jit(solution)/shard_map/ppermute | solution.py:280
  778.2 80.5 %collective-permute-start.40 = (bf16[512,2816]{1,0:T(8,128)(2,1)}, bf16[512,2816]{1,0:T(8,128)(2,1)}, u32[]{:S(2)}, u32[]{:S(2)}) collective-permute-start(bf16[512,2816]{1,0:T(8,128)(2,1)} %pad_maximum_fusion.7), channel_id=1, source_target_pairs={{0,8},{8,0},{16,24},{24,16},{1,9},{9,1},{17,25},{25,17},{2,10},{10... | collective-permute-start | bytes 8650760 | tf_op jit(solution)/shard_map/ppermute | solution.py:283
  788.6 61.8 %collective-permute-start.34 = (bf16[256,1024]{1,0:T(8,128)(2,1)}, bf16[256,1024]{1,0:T(8,128)(2,1)}, u32[]{:S(2)}, u32[]{:S(2)}) collective-permute-start(bf16[256,1024]{1,0:T(8,128)(2,1)} %pad_maximum_fusion.31), channel_id=1, source_target_pairs={{0,8},{8,0},{16,24},{24,16},{1,9},{9,1},{17,25},{25,17},{2,10},{10... | collective-permute-start | bytes 1572872 | tf_op jit(solution)/shard_map/ppermute | solution.py:283
  912.0 96.4 %collective-permute-start.28 = (bf16[512,2048]{1,0:T(8,128)(2,1)}, bf16[512,2048]{1,0:T(8,128)(2,1)}, u32[]{:S(2)}, u32[]{:S(2)}) collective-permute-start(bf16[512,2048]{1,0:T(8,128)(2,1)} %pad_maximum_fusion.16), channel_id=1, source_target_pairs={{0,8},{8,0},{16,24},{24,16},{1,9},{9,1},{17,25},{25,17},{2,10},{10... | collective-permute-start | bytes 6291464 | tf_op jit(solution)/shard_map/ppermute | solution.py:283
  916.3 86.6 %collective-permute-start.21 = (bf16[160,1024]{1,0:T(8,128)(2,1)S(1)}, bf16[160,1024]{1,0:T(8,128)(2,1)}, u32[]{:S(2)}, u32[]{:S(2)}) collective-permute-start(bf16[160,1024]{1,0:T(8,128)(2,1)S(1)} %get-tuple-element.98), channel_id=1, source_target_pairs={{0,0},{2,1},{4,2},{6,3},{1,4},{3,5},{5,6},{7,7},{8,8},{10,9},{12,1... | collective-permute-start | bytes 983048 | tf_op jit(solution)/shard_map/ppermute | solution.py:316
  931.0 73.1 %collective-permute-start.22 = (bf16[160,1024]{1,0:T(8,128)(2,1)}, bf16[160,1024]{1,0:T(8,128)(2,1)}, u32[]{:S(2)}, u32[]{:S(2)}) collective-permute-start(bf16[160,1024]{1,0:T(8,128)(2,1)} %get-tuple-element.97), channel_id=1, source_target_pairs={{1,0},{3,1},{5,2},{7,3},{0,4},{2,5},{4,6},{6,7},{9,8},{11,9},{13,1... | collective-permute-start | bytes 983048 | tf_op jit(solution)/shard_map/ppermute | solution.py:316
  931.9 74.4 %collective-permute-start.16 = (bf16[160,1024]{1,0:T(8,128)(2,1)}, bf16[160,1024]{1,0:T(8,128)(2,1)}, u32[]{:S(2)}, u32[]{:S(2)}) collective-permute-start(bf16[160,1024]{1,0:T(8,128)(2,1)} %get-tuple-element.102), channel_id=1, source_target_pairs={{0,0},{2,1},{4,2},{6,3},{1,4},{3,5},{5,6},{7,7},{8,8},{10,9},{12,1... | collective-permute-start | bytes 983048 | tf_op jit(solution)/shard_map/ppermute | solution.py:316
  933.8 73.6 %collective-permute-start.17 = (bf16[160,1024]{1,0:T(8,128)(2,1)}, bf16[160,1024]{1,0:T(8,128)(2,1)}, u32[]{:S(2)}, u32[]{:S(2)}) collective-permute-start(bf16[160,1024]{1,0:T(8,128)(2,1)} %get-tuple-element.101), channel_id=1, source_target_pairs={{1,0},{3,1},{5,2},{7,3},{0,4},{2,5},{4,6},{6,7},{9,8},{11,9},{13,1... | collective-permute-start | bytes 983048 | tf_op jit(solution)/shard_map/ppermute | solution.py:316
  (140 other events, 1474.4 us)
Sparse Core Ops, SparseCore 0:
  54.7 53.1 all-gather.4
  184.7 63.2 reduce-scatter.4
  249.6 53.9 all-gather.8
  305.6 53.5 all-gather.6
  422.1 50.5 reduce-scatter.8
  479.4 53.4 all-gather.10
  624.3 54.8 all-reduce.3
  681.5 51.3 reduce-scatter.10
  735.3 51.7 reduce-scatter.6

commit v2 on v1

--- a/solution.py
+++ b/solution.py
@@ -262,6 +262,10 @@
     )(queries, keys, values, decays, grads, states, before, entry, exit_grad)
 
 
+def after(value, *others):
+    return lax.optimization_barrier((value, others))[0]
+
+
 class Place:
     def __init__(self):
         self.rows = lax.axis_size("row")
@@ -279,8 +283,16 @@
         n = self.rows
         return lax.ppermute(x, "row", [(i, (i + step) % n) for i in range(n)])
 
-    def swap_group(self, x, bit):
-        return lax.ppermute(x, "dp", [(i, i ^ bit) for i in range(self.groups)])
+    def swap(self, x, axis, bit):
+        return lax.ppermute(x, axis, [(i, i ^ bit) for i in range(lax.axis_size(axis))])
+
+    def sum_over(self, x, *axes):
+        for axis in axes:
+            bit = 1
+            while bit < lax.axis_size(axis):
+                x = x + self.swap(x, axis, bit)
+                bit *= 2
+        return x
 
     def home_pairs(self, k):
         pairs = []
@@ -318,83 +330,120 @@
             out = lax.dynamic_update_slice_in_dim(out, piece, slot * high, 0)
         return out
 
-    def join(self, mine, other, bit):
+    def ordered(self, mine, other, bit):
         high = (self.group & bit) != 0
-        return jnp.concatenate([jnp.where(high, other, mine), jnp.where(high, mine, other)], axis=0)
-
-    def blocks_of(self, own):
-        blocks = [own]
-        high = own.shape[0] // self.groups
-        share = lax.dynamic_slice_in_dim(own, self.group * high, high, 0)
-        for step in range(1, self.rows):
-            part = self.from_row(share, step)
-            bit = 1
-            while bit < self.groups:
-                part = self.join(part, self.swap_group(part, bit), bit)
-                bit *= 2
-            blocks.append(part)
-        return blocks
-
-    def halves(self, x):
-        wide = x.shape[1] // 2
-        bit = self.group & 1
-        keep = lax.dynamic_slice_in_dim(x, bit * wide, wide, 1)
-        send = lax.dynamic_slice_in_dim(x, (1 - bit) * wide, wide, 1)
-        return (keep, send)
-
-    def reduce_weight(self, product):
-        sent = [self.swap_group(part.astype(BF16), 1) for part in product("send")]
-        kept = product("keep")
-        summed = [a + b.astype(F32) for a, b in zip(kept, sent)]
-        own = summed[0]
-        for step in range(1, self.rows):
-            own = own + self.to_row(summed[step].astype(BF16), step).astype(F32)
+        return [jnp.where(high, other, mine), jnp.where(high, mine, other)]
+
+
+class Weight:
+    def __init__(self, place, own, axis):
+        self.place, self.own, self.axis = place, own, axis
+        size = own.shape[axis] // place.groups
+        share, bit = 0, 1
+        while bit < place.groups:
+            share = 2 * share + jnp.where((place.group & bit) != 0, 1, 0)
+            bit *= 2
+        self.share = lax.dynamic_slice_in_dim(own, share * size, size, axis)
+
+    def fetch(self):
+        steps = range(1, self.place.rows)
+        self.parts = [self.place.from_row(self.share, step) for step in steps]
+        return self.parts
+
+    def spread(self):
+        place = self.place
+        bit = place.groups // 2
+        while bit > 1:
+            self.parts = [
+                jnp.concatenate(
+                    place.ordered(part, place.swap(part, "dp", bit), bit), axis=self.axis
+                )
+                for part in self.parts
+            ]
+            bit //= 2
+        return self.parts
+
+    def whole(self):
+        place = self.place
+        pieces = [self.own]
+        for part in self.parts:
+            pieces += place.ordered(part, place.swap(part, "dp", 1), 1)
+        return jnp.concatenate(pieces, axis=self.axis)
+
+
+class Summed:
+    def __init__(self, place, tall):
+        self.place, self.tall = place, tall
+
+    def product(self, tokens, grads):
+        place = self.place
+        bit = place.group & 1
+        blocks = 1 if self.tall else place.rows
+        wide = grads.shape[1] // blocks // 2
+
+        def half(which):
+            parts = [
+                lax.dynamic_slice_in_dim(grads, (2 * i + which) * wide, wide, 1)
+                for i in range(blocks)
+            ]
+            return jnp.concatenate(parts, axis=1) if blocks > 1 else parts[0]
+
+        self.got = place.swap(dot(tokens, half(1 - bit), TN).astype(BF16), "dp", 1)
+        self.kept = dot(tokens, half(bit), TN)
+        return [self.got, self.kept]
+
+    def across(self):
+        rows = self.place.rows
+        total = self.kept + self.got.astype(F32)
+        axis = 0 if self.tall else 1
+        size = total.shape[axis] // rows
+        blocks = [lax.slice_in_dim(total, i * size, (i + 1) * size, axis=axis) for i in range(rows)]
+        self.got = [
+            self.place.to_row(block.astype(BF16), step) for step, block in enumerate(blocks) if step
+        ]
+        self.kept = blocks[0]
+        return self.got
+
+    def along(self):
+        place = self.place
+        own = self.kept
+        for part in self.got:
+            own = own + part.astype(F32)
         bit = 2
-        while bit < self.groups:
+        while bit < place.groups:
             high = own.shape[0] // 2
-            side = jnp.where((self.group & bit) != 0, 1, 0)
+            side = jnp.where((place.group & bit) != 0, 1, 0)
             keep = lax.dynamic_slice_in_dim(own, side * high, high, 0)
             send = lax.dynamic_slice_in_dim(own, (1 - side) * high, high, 0)
-            own = keep + self.swap_group(send.astype(BF16), bit).astype(F32)
+            own = keep + place.swap(send.astype(BF16), "dp", bit).astype(F32)
             bit *= 2
-        own = own.astype(BF16)
-        bit //= 2
-        while bit >= 1:
-            own = self.join(own, self.swap_group(own, bit), bit)
+        self.kept = own.astype(BF16)
+        return self.kept
+
+    def back(self):
+        place = self.place
+        bit = place.groups // 2
+        own = self.kept
+        while bit > 1:
+            own = jnp.concatenate(place.ordered(own, place.swap(own, "dp", bit), bit), axis=0)
             bit //= 2
-        return own.astype(F32)
+        self.kept = own
+        return own
+
+    def finish(self):
+        place = self.place
+        return [
+            part.astype(F32)
+            for part in place.ordered(self.kept, place.swap(self.kept, "dp", 1), 1)
+        ]
 
 
 def gather_tokens(x):
     return lax.all_gather(x, "col", axis=0, tiled=True)
 
 
-def scatter_tokens(parts):
-    return lax.psum_scatter(
-        jnp.concatenate([part.astype(BF16) for part in parts], axis=1),
-        "col",
-        scatter_dimension=0,
-        tiled=True,
-    ).astype(F32)
-
-
-def columns(x, count):
-    wide = x.shape[1] // count
-    return [x[:, i * wide : (i + 1) * wide] for i in range(count)]
-
-
-def over_features(parts, blocks):
-    total = dot(parts[0], blocks[0], NN)
-    for part, block in zip(parts[1:], blocks[1:]):
-        total = total + dot(part, block, NN)
-    return total
-
-
-def over_features_back(parts, blocks):
-    total = dot(parts[0], blocks[0], NT)
-    for part, block in zip(parts[1:], blocks[1:]):
-        total = total + dot(part, block, NT)
-    return total
+def scatter_tokens(part):
+    return lax.psum_scatter(part.astype(BF16), "col", scatter_dimension=0, tiled=True).astype(F32)
 
 
 def norm_factor(values):
@@ -436,85 +485,117 @@
     wide = hidden_in.shape[1]
     rank = rank_down.shape[1]
     head_wide = gain_head.shape[0]
-
-    residual_in = place.to_home(hidden_in).astype(F32)
-    w_in = jnp.concatenate([w_query, w_key, w_value, w_outgate], axis=1)
-    w_two = jnp.concatenate([w_gate, w_up], axis=1)
-    in_blocks = place.blocks_of(w_in)
+    hidden_wide = w_gate.shape[1]
+    value_end = 2 * HEAD_K + HEAD_V
+
     small = jnp.concatenate([gain_attn, gain_ffn, gain_head, rank_down.reshape(-1)])
     smalls = [small] + [place.from_row(small, step) for step in range(1, rows)]
+    home_in = place.to_home(hidden_in)
+    residual_in = home_in.astype(F32)
+    weight_in = Weight(
+        place,
+        jnp.concatenate([w_query, w_key, w_value, w_outgate], axis=1),
+        0,
+    )
+    weight_out = Weight(place, w_output, 1)
+    weight_down = Weight(place, w_down, 1)
+    weight_two = Weight(place, jnp.concatenate([w_gate, w_up], axis=1), 0)
+    weight_in.share = after(weight_in.share, home_in)
+    got_in = weight_in.fetch()
+    home_cot = place.to_home(after(cotangent, home_in))
+    for weight in (weight_out, weight_down, weight_two):
+        weight.share = after(weight.share, *got_in)
+    got_out = weight_out.fetch()
+    got_down = weight_down.fetch()
+    got_two = weight_two.fetch()
+    weight_in.spread()
+    w_in = weight_in.whole()
+
     gain_one = jnp.concatenate([s[:wide] for s in smalls]).astype(F32)
     gain_two = jnp.concatenate([s[wide : 2 * wide] for s in smalls]).astype(F32)
     heads = jnp.stack([s[2 * wide : 2 * wide + head_wide] for s in smalls])
     gain_mix = jnp.roll(heads, place.row, axis=0).reshape(-1).astype(F32)
-    down_blocks = [s[2 * wide + head_wide :].reshape(wide, rank) for s in smalls]
+    w_rank = jnp.concatenate(
+        [s[2 * wide + head_wide :].reshape(wide, rank) for s in smalls], axis=0
+    )
 
     place_home = place.row * half_rows + place.col * home_rows
     valid = (place_home + jnp.arange(home_rows) < seq_lengths[0]).astype(F32)[:, None]
+    upstream = valid * home_cot.astype(F32)
 
     factor_one = norm_factor(residual_in)
     normed_one = (residual_in * factor_one * gain_one).astype(BF16)
     tokens_one = gather_tokens(normed_one)
-    ones = columns(tokens_one, rows)
-    pre = over_features(ones, in_blocks)
+    ffn_grad = gather_tokens(after(upstream.astype(BF16), normed_one))
+    tokens_one = after(tokens_one, w_in, upstream, *got_out, *got_down)
+    pre = dot(tokens_one, w_in, NN)
     queries = pre[:, :HEAD_K].astype(BF16)
     keys = pre[:, HEAD_K : 2 * HEAD_K].astype(BF16)
-    values = pre[:, 2 * HEAD_K : 2 * HEAD_K + HEAD_V].astype(BF16)
-    outgate = pre[:, 2 * HEAD_K + HEAD_V :]
-    rank_mid = over_features(ones, down_blocks).astype(BF16)
+    values = pre[:, 2 * HEAD_K : value_end].astype(BF16)
+    outgate = pre[:, value_end:]
+    rank_mid = dot(tokens_one, w_rank, NN).astype(BF16)
     decay_logits = dot(rank_mid, rank_up, NN) + decay_bias
     decays = jax.nn.log_sigmoid(decay_logits) / 16.0
+    decays = after(decays, *got_two)
 
     ending = attend_state(keys, values, decays)
     steps = [(i, i + 1) for i in range(rows - 1)]
-    entry = lax.ppermute(ending, "row", steps)
+    entry = lax.ppermute(ending.astype(BF16), "row", steps).astype(F32)
     if rows > 2:
         all_fade = jnp.exp(jnp.sum(decays, axis=0))[None, :]
         for _ in range(rows - 2):
-            entry = lax.ppermute(entry * all_fade + ending, "row", steps)
+            entry = lax.ppermute((entry * all_fade + ending).astype(BF16), "row", steps).astype(F32)
     mixed, faded, states, before = attend_forward(queries, keys, values, decays)
+    weight_out.spread()
+    spread_down = weight_down.spread()
+    spread_two = weight_two.spread()
+    w_out = weight_out.whole()
+    mixed = after(mixed, w_out)
     mixed = mixed + dot(faded, entry, NT, HIGH)
     factor_head = norm_factor(mixed)
     normed_head = mixed * factor_head * gain_mix
     out_sig = jax.nn.sigmoid(outgate)
     out_act = outgate * out_sig
     gated = (normed_head * out_act).astype(BF16)
-    out_blocks = place.blocks_of(w_output)
-    attn_out = scatter_tokens([dot(gated, block, NN) for block in out_blocks])
+    gated = after(gated, ffn_grad, *spread_down, *spread_two)
+    attn_out = scatter_tokens(dot(gated, w_out, NN))
+    w_ffn = weight_down.whole()
+    w_two = weight_two.whole()
+    hidden_grad = dot(ffn_grad, w_ffn, NT)
+    attn_out = after(attn_out, hidden_grad, w_two)
     residual_mid = residual_in + attn_out
 
     factor_two = norm_factor(residual_mid)
     normed_two = (residual_mid * factor_two * gain_two).astype(BF16)
     tokens_two = gather_tokens(normed_two)
-    twos = columns(tokens_two, rows)
-    two_blocks = place.blocks_of(w_two)
-    both = over_features(twos, two_blocks)
-    hidden_wide = w_gate.shape[1]
+    both = dot(tokens_two, w_two, NN)
     gate_pre = both[:, :hidden_wide]
     up_pre = both[:, hidden_wide:]
     swish_sig = jax.nn.sigmoid(gate_pre)
     swish_out = gate_pre * swish_sig
     hidden = (swish_out * up_pre).astype(BF16)
-    ffn_blocks = place.blocks_of(w_down)
-
-    upstream = valid * place.to_home(cotangent).astype(F32)
-    ffn_grad = gather_tokens(upstream.astype(BF16))
-    ffn_grads = columns(ffn_grad, rows)
-    hidden_grad = over_features_back(ffn_grads, ffn_blocks)
     swish_slope = swish_sig * (1.0 + gate_pre * (1.0 - swish_sig))
     gate_grad = (hidden_grad * up_pre * swish_slope).astype(BF16)
     up_grad = (hidden_grad * swish_out).astype(BF16)
     both_grad = jnp.concatenate([gate_grad, up_grad], axis=1)
-
-    normed_two_grad = scatter_tokens([dot(both_grad, block, NT) for block in two_blocks])
+    normed_two_grad = scatter_tokens(dot(both_grad, w_two, NT))
+
+    sum_two = Summed(place, True)
+    sum_down = Summed(place, False)
+    held = sum_down.product(hidden, ffn_grad) + sum_two.product(tokens_two, both_grad)
+    across_down = sum_down.across()
+    across_two = sum_two.across()
+    normed_two_grad = after(normed_two_grad, *held)
+
     mid_part, gain_two_grad = norm_backward(residual_mid, factor_two, gain_two, normed_two_grad)
     mid_grad = upstream + mid_part
-    ffn_out = scatter_tokens([dot(hidden, block, NN) for block in ffn_blocks])
-    block_out = place.from_home((valid * (residual_mid + ffn_out)).astype(BF16))
-
     attn_grad = gather_tokens(mid_grad.astype(BF16))
-    attn_grads = columns(attn_grad, rows)
-    gated_grad = over_features_back(attn_grads, out_blocks)
+    attn_grad = after(attn_grad, *across_down, *across_two)
+    along_down = sum_down.along()
+    along_two = sum_two.along()
+
+    gated_grad = dot(attn_grad, w_out, NT)
+    ffn_out = scatter_tokens(dot(after(hidden, attn_grad), w_ffn, NN))
     head_grad = gated_grad * out_act
     out_slope = out_sig * (1.0 + outgate * (1.0 - out_sig))
     outgate_grad = (gated_grad * normed_head * out_slope).astype(BF16)
@@ -522,78 +603,97 @@
 
     start_grad = dot(mixed_grad, faded, TN, HIGH)
     back = [(i + 1, i) for i in range(rows - 1)]
-    exit_grad = lax.ppermute(start_grad, "row", back)
+    exit_grad = lax.ppermute(start_grad.astype(BF16), "row", back).astype(F32)
     if rows > 2:
         for _ in range(rows - 2):
-            exit_grad = lax.ppermute(exit_grad * all_fade + start_grad, "row", back)
+            exit_grad = lax.ppermute(
+                (exit_grad * all_fade + start_grad).astype(BF16), "row", back
+            ).astype(F32)
+    sum_out = Summed(place, False)
+    sum_gate = Summed(place, True)
+    held = sum_out.product(gated, attn_grad) + sum_gate.product(tokens_one, outgate_grad)
+    exit_grad = after(exit_grad, along_down, along_two, *held)
     query_grad, key_grad, value_grad, decay_grad = attend_backward(
         queries, keys, values, decays, mixed_grad, states, before, entry, exit_grad
     )
+    across_out = sum_out.across()
+    across_gate = sum_gate.across()
+    back_down = sum_down.back()
+    back_two = sum_two.back()
+    in_grad = jnp.concatenate([query_grad, key_grad, value_grad, outgate_grad], axis=1)
+    in_grad = after(in_grad, back_down, back_two, *across_out, *across_gate)
+    one_part = dot(in_grad, w_in, NT)
+    normed_one_grad = scatter_tokens(one_part)
+
+    sums = [Summed(place, True) for _ in range(3)]
+    for total, grads in zip(sums, (query_grad, key_grad, value_grad)):
+        total.product(tokens_one, after(grads, one_part))
     logit_grad = decay_grad * jax.nn.sigmoid(-decay_logits) / 16.0
     rank_up_part = dot(rank_mid.astype(F32), logit_grad, TN, HIGHEST)
     bias_part = jnp.sum(logit_grad, axis=0)
-    rank_term = dot(logit_grad, rank_up.astype(F32), NT, HIGHEST)
-    rank_grad = lax.psum(rank_term, "col").astype(BF16)
-    in_grad = jnp.concatenate([query_grad, key_grad, value_grad, outgate_grad], axis=1)
-    normed_one_grad = scatter_tokens([dot(in_grad, block, NT) for block in in_blocks])
-    own_rank = lax.dynamic_slice_in_dim(rank_grad, place.col * home_rows, home_rows, 0)
-    normed_one_grad = normed_one_grad + jnp.concatenate(
-        [dot(own_rank, block, NT) for block in down_blocks], axis=1
-    )
+    rank_term = dot(rank_up.astype(F32), logit_grad, NT, HIGHEST)
+    rank_grad = place.sum_over(rank_term, "col").astype(BF16)
+    rank_down_part = dot(rank_grad, tokens_one, NN)
+
+    def absolute(x):
+        return jnp.roll(x.reshape((rows, -1)), place.row, axis=0).reshape(-1)
+
+    decay_flat = jnp.concatenate(
+        [rank_up_part.reshape(-1), bias_part]
+        + [absolute(rank_down_part[i]) for i in range(rank)]
+    )
+    decay_flat = place.sum_over(decay_flat, "dp", "row")
+
+    for total in sums:
+        total.across()
+    grads_out = []
+    for total in (sum_out, sum_gate, *sums):
+        total.along()
+    for total in (sum_down, sum_two):
+        grads_out.append(total.finish())
+    for total in (sum_out, sum_gate, *sums):
+        total.back()
+        grads_out.append(total.finish())
+    grad_down, (grad_gate, grad_up), grad_out, grad_og, grad_q, grad_k, grad_v = grads_out
+    block_out = place.from_home((valid * (residual_mid + ffn_out)).astype(BF16))
+
+    own_rank = lax.dynamic_slice_in_dim(rank_grad, place.col * home_rows, home_rows, 1)
+    normed_one_grad = normed_one_grad + dot(own_rank, w_rank, (((0,), (1,)), ((), ())))
     input_part, gain_one_grad = norm_backward(residual_in, factor_one, gain_one, normed_one_grad)
     grad_input = place.from_home((mid_grad + input_part).astype(BF16)).astype(F32)
-
-    def tall(tokens, grads):
-        def product(which):
-            pick = 0 if which == "keep" else 1
-            return [dot(place.halves(x)[pick], grads, TN) for x in columns(tokens, rows)]
-
-        return place.reduce_weight(product)
-
-    def broad(left, grads):
-        def product(which):
-            pick = 0 if which == "keep" else 1
-            return columns(dot(place.halves(left)[pick], grads, TN), rows)
-
-        return place.reduce_weight(product)
-
-    grad_down = broad(hidden, ffn_grad)
-    grad_two = tall(tokens_two, both_grad)
-    grad_output = broad(gated, attn_grad)
-    grad_in = tall(tokens_one, in_grad)
-
-    def absolute(x):
-        return jnp.roll(x.reshape((rows, -1) + x.shape[1:]), place.row, axis=0).reshape(x.shape)
-
-    down_part = jnp.concatenate([dot(x, rank_grad, TN) for x in ones], axis=0)
-    decay_all = lax.psum(
-        (rank_up_part, bias_part, absolute(down_part)), ("dp", "row")
-    )
-    gains_all = lax.psum(
-        (absolute(gain_one_grad), gain_mix_grad, absolute(gain_two_grad)), ("dp", "row", "col")
-    )
+    gains = jnp.concatenate([absolute(gain_one_grad), absolute(gain_two_grad), gain_mix_grad])
+    gains = place.sum_over(gains, "dp", "row", "col")
 
     def mine(x):
         size = x.shape[0] // rows
         return lax.dynamic_slice_in_dim(x, place.row * size, size, 0)
 
+    model = wide * rows
+    ups = rank * rank_up.shape[1]
+    bias_end = ups + decay_bias.shape[0]
+    rank_out = decay_flat[bias_end:].reshape(rank, model)
+    rank_out = lax.dynamic_slice_in_dim(rank_out, place.row * wide, wide, 1).T
+
+    def columns(pair):
+        return jnp.concatenate(pair, axis=1)
+
     return (
         block_out,
         grad_input,
-        mine(gains_all[0]),
-        grad_in[:, :HEAD_K],
-        grad_in[:, HEAD_K : 2 * HEAD_K],
-        grad_in[:, 2 * HEAD_K : 2 * HEAD_K + HEAD_V],
-        grad_in[:, 2 * HEAD_K + HEAD_V :],
-        mine(decay_all[2]),
-        decay_all[0],
-        decay_all[1],
-        mine(gains_all[1]),
-        grad_output,
-        mine(gains_all[2]),
-        grad_two[:, :hidden_wide],
-        grad_two[:, hidden_wide:],
-        grad_down,
+        mine(gains[:model]),
+        columns(grad_q),
+        columns(grad_k),
+        columns(grad_v),
+        columns(grad_og),
+        rank_out,
+        decay_flat[:ups].reshape(rank, -1),
+        decay_flat[ups:bias_end],
+        mine(gains[2 * model :]),
+        columns(grad_out),
+        mine(gains[model : 2 * model]),
+        grad_gate,
+        grad_up,
+        columns(grad_down),
     )
 
 

time: 1030 us -> 806 us (0.78)
  blocking collectives: 134 us -> 0 us
  waiting for transfers between devices: 439 us -> 368 us
  local copies, waits for them, and re-layouts: 82.1 us -> 59 us
  matrix products: 133 us -> 116 us
  starting transfers between devices: 55.5 us -> 69.8 us
    psum x3 -> x0, blocking collectives: 134 us -> none  [the longest x1 63.1 us: body(): lax.psum((absolute(gain_one_grad), gain_mix_grad, absolute(gain_two_grad)...]
    ppermute x30 -> x48, waiting for transfers between devices: 240 us -> 116 us  [the longest x46 116 us: swap(): lax.ppermute(x, axis, [(i, i ^ bit) for i in range(lax.axis_size(axis))])]
    ppermute x4 -> x7, waiting for transfers between devices: 21.6 us -> 116 us  [to_row(): return lax.ppermute(x, 'row', [(i, (i + step) % n) for i in range(n)])]
    reduce_scatter x4, waiting for transfers between devices: 50.5 us -> 17.8 us  [scatter_tokens(): lax.psum_scatter(part.astype(BF16), 'col', scatter_dimension=0, tiled=True)]
    concatenate x14 -> x21, other arithmetic: 20.4 us -> 48.2 us  [the longest x2 24.4 us: whole(): return jnp.concatenate(pieces, axis=self.axis)]
    ppermute x4, waiting for transfers between devices: 0.01 us -> 19.3 us  [from_home(): piece = lax.ppermute(piece, ('row', 'col'), pairs)]
    ppermute x4, waiting for transfers between devices: 39 us -> 19.9 us  [to_home(): piece = lax.ppermute(piece, ('row', 'col'), self.home_pairs(k))]
    dot_general x39 -> x30, matrix products: 133 us -> 116 us  [dot(): lax.dot_general(left, right, dims, precision=precision, preferred_element...]
  transfers between devices with their start and end apart: 56 -> 76, of which waited for: 21 -> 32; matrix products, arithmetic and copies ran while one was open for 24% -> 30% of each run, Pallas kernels for 5% -> 6%
where the time goes in v2:
time: 806 us; the launch traced here: 796 us
  waiting for transfers between devices  368 us (46%)
  other arithmetic  117 us (15%)
  matrix products  116 us (14%)
  starting transfers between devices  69.8 us (9%)
  local copies, waits for them, and re-layouts  59 us (7%)
  Pallas kernels  48.2 us (6%)
  between operations  17.5 us (2%)
    ppermute x46, waiting for transfers between devices, swap(): lax.ppermute(x, axis, [(i, i ^ bit) for i in range(lax.axis_size(axis))])  116 us
    dot_general x30, matrix products, dot(): lax.dot_general(left, right, dims, precision=precision, preferred_element...  116 us
    ppermute x7, waiting for transfers between devices, to_row(): return lax.ppermute(x, 'row', [(i, (i + step) % n) for i in range(n)])  116 us
    all_gather x4, waiting for transfers between devices, gather_tokens(): return lax.all_gather(x, 'col', axis=0, tiled=True)  50.2 us
    ppermute x46, starting transfers between devices, swap(): lax.ppermute(x, axis, [(i, i ^ bit) for i in range(lax.axis_size(axis))])  32.1 us
    ppermute x5, waiting for transfers between devices, from_row(): return lax.ppermute(x, 'row', [((i + step) % n, i) for i in range(n)])  29.6 us
    concatenate x2, other arithmetic, whole(): return jnp.concatenate(pieces, axis=self.axis)  24.4 us
    pallas_call x1, Pallas kernels, attend_backward(): pl.pallas_call(backward_kernel, grid=(count,), in_specs=[row_k, row_k, ro...  22.7 us
  transfers between devices with their start and end apart: 76, of which 32 were waited for; matrix products, arithmetic and copies ran while one was open for 30% of the time, Pallas kernels for 6%

profile of v2, /device:TPU:10, one launch (start us, length us, event | category | flops | bytes accessed | tf_op | source)
XLA Modules:
  0.0 795.8 jit_solution(4983217341310130909)
XLA Ops:
  37.2 17.0 %collective-permute-done.3 = bf16[256,2048]{1,0:T(8,128)(2,1)S(1)} collective-permute-done((bf16[256,2048]{1,0:T(8,128)(2,1)S(1)}, bf16[256,2048]{1,0:T(8,128)(2,1)S(1)}, u32[]{:S(2)}, u32[]{:S(2)}) %collective-permute-start.3) | collective-permute-done | bytes 1048608 | tf_op jit(solution)/shard_map/ppermute | solution.py:280
  70.8 9.6 %collective-permute-done.4 = bf16[256,2048]{1,0:T(8,128)(2,1)} collective-permute-done((bf16[256,2048]{1,0:T(8,128)(2,1)S(1)}, bf16[256,2048]{1,0:T(8,128)(2,1)}, u32[]{:S(2)}, u32[]{:S(2)}) %collective-permute-start.4) | collective-permute-done | bytes 1048608 | tf_op jit(solution)/shard_map/ppermute | solution.py:287
  83.5 6.3 collective-permute-done.6
  90.8 9.8 %collective-permute-done.7 = bf16[160,1024]{1,0:T(8,128)(2,1)S(1)} collective-permute-done((bf16[160,1024]{1,0:T(8,128)(2,1)S(1)}, bf16[160,1024]{1,0:T(8,128)(2,1)S(1)}, u32[]{:S(2)}, u32[]{:S(2)}) %collective-permute-start.7) | collective-permute-done | bytes 327712 | tf_op jit(solution)/shard_map/ppermute | solution.py:314
  105.5 13.2 %collective-permute-done.14 = bf16[1408,256]{1,0:T(8,128)(2,1)} collective-permute-done((bf16[1408,256]{1,0:T(8,128)(2,1)}, bf16[1408,256]{1,0:T(8,128)(2,1)}, u32[]{:S(2)}, u32[]{:S(2)}) %collective-permute-start.14) | collective-permute-done | bytes 720928 | tf_op jit(solution)/shard_map/ppermute | solution.py:287
  121.6 12.6 %collective-permute-done.10 = bf16[256,2816]{1,0:T(8,128)(2,1)} collective-permute-done((bf16[256,2816]{1,0:T(8,128)(2,1)}, bf16[256,2816]{1,0:T(8,128)(2,1)}, u32[]{:S(2)}, u32[]{:S(2)}) %collective-permute-start.10) | collective-permute-done | bytes 1441824 | tf_op jit(solution)/shard_map/ppermute | solution.py:280
  147.6 9.5 %fusion.119 = (bf16[640,2048]{1,0:T(8,128)(2,1)S(1)}, f32[640,2048]{1,0:T(8,128)}) fusion(bf16[640,2048]{1,0:T(8,128)(2,1)S(1)} %copy-done.13, bf16[2048,2048]{1,0:T(8,128)(2,1)} %pad_maximum_fusion.1), kind=kOutput, calls=%fused_computation.391 | convolution fusion | flops 5370019840 | bytes 18874368 | tf_op jit(solution)/shard_map/dot_general | solution.py:25
  158.5 9.9 %recurrence_state.1 = f32[512,512]{1,0:T(8,128)} custom-call(bf16[640,512]{1,0:T(8,128)(2,1)} %get-tuple-element.129.k_ref, bf16[640,512]{1,0:T(8,128)(2,1)} %get-tuple-element.128.v_ref, f32[640,512]{1,0:T(8,128)} %get-tuple-element.50.decay_ref), custom_call_target="tpu_custom_call" | custom-call | tf_op jit(solution)/shard_map/recurrence_state/pallas_call | solution.py:219
  175.5 15.6 %recurrence_forward.1 = (f32[640,512]{1,0:T(8,128)}, f32[640,512]{1,0:T(8,128)}, f32[10,512,512]{2,1,0:T(8,128)}, f32[10,8,512]{2,1,0:T(8,128)}) custom-call(bf16[640,512]{1,0:T(8,128)(2,1)} %get-tuple-element.130.q_ref, bf16[640,512]{1,0:T(8,128)(2,1)} %get-tuple-element.129.k_ref, bf16[640,512]{1,0:T(8,128)(2,1)} %get-tuple-element.128.v_ref, ...), custom_call_target="tpu_custom_call" | custom-call | tf_op jit(solution)/shard_map/recurrence_forward/pallas_call | solution.py:191
  208.1 6.1 fusion.3
  215.4 20.4 %pad_maximum_fusion = bf16[2048,2816]{1,0:T(8,128)(2,1)} fusion(bf16[512,2816]{1,0:T(8,128)(2,1)S(1)} %get-tuple-element.109, bf16[512,2816]{1,0:T(8,128)(2,1)S(1)} %get-tuple-element.108, bf16[1024,2816]{1,0:T(8,128)(2,1)S(1)} %bitcast.127), kind=kLoop, calls=%fused_computation | loop fusion | flops 34603008 | bytes 23068672 | tf_op jit(solution)/shard_map/concatenate | solution.py:371
  235.7 17.8 %reduce-scatter.5.cloned.1.call-done = bf16[160,2048]{1,0:T(8,128)(2,1)} async-done(((bf16[640,2048]{1,0:T(8,128)(2,1)}), bf16[160,2048]{1,0:T(8,128)(2,1)}) %reduce-scatter.5.cloned.1.call-update) | async-done | bytes 655376 | tf_op jit(solution)/shard_map/reduce_scatter | solution.py:446
  259.5 50.2 %all-gather.9.cloned.1.call-done = bf16[640,2048]{1,0:T(8,128)(2,1)} async-done(((bf16[160,2048]{1,0:T(8,128)(2,1)}), bf16[640,2048]{1,0:T(8,128)(2,1)}) %all-gather.9.cloned.1.call-update) | async-done | bytes 2621456 | tf_op jit(solution)/shard_map/all_gather | solution.py:442
  309.7 12.0 %fusion.120 = f32[640,2816]{1,0:T(8,128)S(1)} fusion(bf16[640,2048]{1,0:T(8,128)(2,1)} %all-gather.9.cloned.1.call-done, bf16[2048,2816]{1,0:T(8,128)(2,1)} %pad_maximum_fusion), kind=kOutput, calls=%fused_computation.392 | convolution fusion | flops 7381975040 | bytes 21364736 | tf_op jit(solution)/shard_map/dot_general | solution.py:25
  328.2 7.0 convolution_convert_fusion
  335.7 9.0 %fusion.2 = bf16[640,2048]{1,0:T(8,128)(2,1)} fusion(bf16[2048,2816]{1,0:T(8,128)(2,1)S(1)} %bitcast.129, bf16[640,1408]{1,0:T(8,128)(2,1)S(1)} %get-tuple-element.102, bf16[640,1408]{1,0:T(8,128)(2,1)S(1)} %get-tuple-element.101), kind=kOutput, calls=%fused_computation.21 | convolution fusion | flops 7390494720 | bytes 17760256 | tf_op jit(solution)/shard_map/dot_general | solution.py:25
  354.0 33.2 %collective-permute-done.20 = bf16[1408,512]{1,0:T(8,128)(2,1)S(1)} collective-permute-done((bf16[1408,512]{1,0:T(8,128)(2,1)}, bf16[1408,512]{1,0:T(8,128)(2,1)S(1)}, u32[]{:S(2)}, u32[]{:S(2)}) %collective-permute-start.20) | collective-permute-done | bytes 1441824 | tf_op jit(solution)/shard_map/ppermute | solution.py:284
  392.8 15.9 %collective-permute-done.25 = bf16[704,512]{1,0:T(8,128)(2,1)S(1)} collective-permute-done((bf16[704,512]{1,0:T(8,128)(2,1)S(1)}, bf16[704,512]{1,0:T(8,128)(2,1)S(1)}, u32[]{:S(2)}, u32[]{:S(2)}) %collective-permute-start.25) | collective-permute-done | bytes 720928 | tf_op jit(solution)/shard_map/ppermute | solution.py:287
  413.0 8.1 %convert_add_fusion = f32[2048,1408]{1,0:T(8,128)S(1)} fusion(bf16[2048,1408]{1,0:T(8,128)(2,1)} %collective-permute-done.19, bf16[640,2048]{1,0:T(8,128)(2,1)} %all-gather.9.cloned.1.call-done, s32[]{:T(128)S(6)} %select_n.467, bf16[640,1408]{1,0:T(8,128)(2,1)} %copy-done.42, bf16[640,1408]{1,0:T(8,128)(2,1)} %copy-done.43), kind=kOutput, calls=%fused_computation.1 | convolution fusion | flops 3700359168 | bytes 23527428 | tf_op jit(solution)/shard_map/dot_general | solution.py:25
  436.9 49.4 %collective-permute-done.21 = bf16[1024,1408]{1,0:T(8,128)(2,1)} collective-permute-done((bf16[1024,1408]{1,0:T(8,128)(2,1)}, bf16[1024,1408]{1,0:T(8,128)(2,1)}, u32[]{:S(2)}, u32[]{:S(2)}) %collective-permute-start.21) | collective-permute-done | bytes 2883616 | tf_op jit(solution)/shard_map/ppermute | solution.py:284
  510.6 14.4 %collective-permute-done.26 = bf16[512,1408]{1,0:T(8,128)(2,1)} collective-permute-done((bf16[512,1408]{1,0:T(8,128)(2,1)}, bf16[512,1408]{1,0:T(8,128)(2,1)}, u32[]{:S(2)}, u32[]{:S(2)}) %collective-permute-start.26) | collective-permute-done | bytes 1441824 | tf_op jit(solution)/shard_map/ppermute | solution.py:287
  533.1 22.7 %recurrence_backward.1 = (bf16[640,512]{1,0:T(8,128)(2,1)}, bf16[640,512]{1,0:T(8,128)(2,1)}, bf16[640,512]{1,0:T(8,128)(2,1)}, f32[640,512]{1,0:T(8,128)}) custom-call(bf16[640,512]{1,0:T(8,128)(2,1)} %get-tuple-element.130.q_ref, bf16[640,512]{1,0:T(8,128)(2,1)} %get-tuple-element.129.k_ref, bf16[640,512]{1,0:T(8,128)(2,1)} %get-tuple-element.128.v_ref, ...), custom_call_target="tpu_custom_call" | custom-call | tf_op jit(solution)/shard_map/recurrence_backward/pallas_call | solution.py:238
  584.1 10.3 %fusion.121 = bf16[640,2048]{1,0:T(8,128)(2,1)} fusion(bf16[640,2048]{1,0:T(8,128)(2,1)S(1)} %copy-done.37, bf16[2048,2048]{1,0:T(8,128)(2,1)} %pad_maximum_fusion.1), kind=kOutput, calls=%fused_computation.393 | convolution fusion | flops 5368709120 | bytes 13631488 | tf_op jit(solution)/shard_map/dot_general | solution.py:25
  602.0 6.0 convolution_convert_fusion.2
  652.1 9.0 %collective-permute-done.43 = bf16[1024,256]{1,0:T(8,128)(2,1)S(1)} collective-permute-done((bf16[1024,256]{1,0:T(8,128)(2,1)S(1)}, bf16[1024,256]{1,0:T(8,128)(2,1)S(1)}, u32[]{:S(2)}, u32[]{:S(2)}) %collective-permute-start.43) | collective-permute-done | bytes 524320 | tf_op jit(solution)/shard_map/ppermute | solution.py:284
  662.1 10.3 %collective-permute-done.48 = bf16[1024,256]{1,0:T(8,128)(2,1)S(1)} collective-permute-done((bf16[1024,256]{1,0:T(8,128)(2,1)S(1)}, bf16[1024,256]{1,0:T(8,128)(2,1)S(1)}, u32[]{:S(2)}, u32[]{:S(2)}) %collective-permute-start.48) | collective-permute-done | bytes 524320 | tf_op jit(solution)/shard_map/ppermute | solution.py:284
  673.3 9.5 %collective-permute-done.53 = bf16[1024,256]{1,0:T(8,128)(2,1)S(1)} collective-permute-done((bf16[1024,256]{1,0:T(8,128)(2,1)S(1)}, bf16[1024,256]{1,0:T(8,128)(2,1)S(1)}, u32[]{:S(2)}, u32[]{:S(2)}) %collective-permute-start.53) | collective-permute-done | bytes 524320 | tf_op jit(solution)/shard_map/ppermute | solution.py:284
  686.0 6.2 collective-permute-done.54
  698.0 5.5 collective-permute-done.50
  731.1 7.0 select_convert_fusion
  745.3 19.7 %collective-permute-done.41 = f32[4608]{0:T(1024)S(1)} collective-permute-done((f32[4608]{0:T(1024)S(1)}, f32[4608]{0:T(1024)S(1)}, u32[]{:S(2)}, u32[]{:S(2)}) %collective-permute-start.41) | collective-permute-done | bytes 18464 | tf_op jit(solution)/shard_map/ppermute | solution.py:287
  767.0 19.3 %collective-permute-done.36 = bf16[160,1024]{1,0:T(8,128)(2,1)S(1)} collective-permute-done((bf16[160,1024]{1,0:T(8,128)(2,1)S(1)}, bf16[160,1024]{1,0:T(8,128)(2,1)S(1)}, u32[]{:S(2)}, u32[]{:S(2)}) %collective-permute-start.36) | collective-permute-done | bytes 327712 | tf_op jit(solution)/shard_map/ppermute | solution.py:328
  (580 shorter events, 306.2 us)
Async XLA Ops:
  7.2 135.3 %all-gather.5.cloned.1.call-start = ((), (), s32[]{:S(2)}) async-start(), calls=%async_computation.4 | async-start | bytes 3276800 | tf_op jit(solution)/shard_map/all_gather | solution.py:442
  30.1 24.1 %collective-permute-start.3 = (bf16[256,2048]{1,0:T(8,128)(2,1)S(1)}, bf16[256,2048]{1,0:T(8,128)(2,1)S(1)}, u32[]{:S(2)}, u32[]{:S(2)}) collective-permute-start(bf16[256,2048]{1,0:T(8,128)(2,1)S(1)} %constant_dynamic-slice_fusion.58), channel_id=1, source_target_pairs={{4,0},{0,4},{5,1},{1,5},{6,2},{2,6},{7,3},{3,7},{12,8},{8,12},{13,... | collective-permute-start | bytes 3145736 | tf_op jit(solution)/shard_map/ppermute | solution.py:280
  31.3 166.6 %all-gather.7.cloned.1.call-start = ((), (), s32[]{:S(2)}) async-start(), calls=%async_computation.5 | async-start | bytes 3276800 | tf_op jit(solution)/shard_map/all_gather | solution.py:442
  54.2 26.1 %collective-permute-start.4 = (bf16[256,2048]{1,0:T(8,128)(2,1)S(1)}, bf16[256,2048]{1,0:T(8,128)(2,1)}, u32[]{:S(2)}, u32[]{:S(2)}) collective-permute-start(bf16[256,2048]{1,0:T(8,128)(2,1)S(1)} %collective-permute-done.3), channel_id=1, source_target_pairs={{0,16},{8,24},{16,0},{24,8},{1,17},{9,25},{17,1},{25,9},{2,18},{10... | collective-permute-start | bytes 3145736 | tf_op jit(solution)/shard_map/ppermute | solution.py:287
  62.4 27.4 %collective-permute-start.6 = (bf16[160,1024]{1,0:T(8,128)(2,1)S(1)}, bf16[160,1024]{1,0:T(8,128)(2,1)S(1)}, u32[]{:S(2)}, u32[]{:S(2)}) collective-permute-start(bf16[160,1024]{1,0:T(8,128)(2,1)S(1)} %get-tuple-element.154), channel_id=1, source_target_pairs={{0,0},{1,2},{2,4},{3,6},{4,1},{5,3},{6,5},{7,7},{8,8},{9,10},{10,1... | collective-permute-start | bytes 983048 | tf_op jit(solution)/shard_map/ppermute | solution.py:314
  66.0 34.6 %collective-permute-start.7 = (bf16[160,1024]{1,0:T(8,128)(2,1)S(1)}, bf16[160,1024]{1,0:T(8,128)(2,1)S(1)}, u32[]{:S(2)}, u32[]{:S(2)}) collective-permute-start(bf16[160,1024]{1,0:T(8,128)(2,1)S(1)} %get-tuple-element.153), channel_id=1, source_target_pairs={{0,1},{1,3},{2,5},{3,7},{4,0},{5,2},{6,4},{7,6},{8,9},{9,11},{10,1... | collective-permute-start | bytes 983048 | tf_op jit(solution)/shard_map/ppermute | solution.py:314
  67.4 33.3 %collective-permute-start.9 = (bf16[1408,256]{1,0:T(8,128)(2,1)}, bf16[1408,256]{1,0:T(8,128)(2,1)}, u32[]{:S(2)}, u32[]{:S(2)}) collective-permute-start(bf16[1408,256]{1,0:T(8,128)(2,1)} %constant_dynamic-slice_fusion.54), channel_id=1, source_target_pairs={{4,0},{0,4},{5,1},{1,5},{6,2},{2,6},{7,3},{3,7},{12,8},{8,12},{13,... | collective-permute-start | bytes 2162696 | tf_op jit(solution)/shard_map/ppermute | solution.py:280
  83.5 52.2 %collective-permute-start.5 = (bf16[512,2048]{1,0:T(8,128)(2,1)}, bf16[512,2048]{1,0:T(8,128)(2,1)}, u32[]{:S(2)}, u32[]{:S(2)}) collective-permute-start(bf16[512,2048]{1,0:T(8,128)(2,1)} %pad_maximum_fusion.12), channel_id=1, source_target_pairs={{0,8},{8,0},{16,24},{24,16},{1,9},{9,1},{17,25},{25,17},{2,10},{10... | collective-permute-start | bytes 6291464 | tf_op jit(solution)/shard_map/ppermute | solution.py:287
  100.6 33.5 %collective-permute-start.10 = (bf16[256,2816]{1,0:T(8,128)(2,1)}, bf16[256,2816]{1,0:T(8,128)(2,1)}, u32[]{:S(2)}, u32[]{:S(2)}) collective-permute-start(bf16[256,2816]{1,0:T(8,128)(2,1)} %constant_dynamic-slice_fusion.53), channel_id=1, source_target_pairs={{4,0},{0,4},{5,1},{1,5},{6,2},{2,6},{7,3},{3,7},{12,8},{8,12},{13,... | collective-permute-start | bytes 4325384 | tf_op jit(solution)/shard_map/ppermute | solution.py:280
  103.3 150.2 %reduce-scatter.5.cloned.1.call-start = ((), (), s32[]{:S(2)}) async-start(), calls=%async_computation.6 | async-start | bytes 3276800 | tf_op jit(solution)/shard_map/reduce_scatter | solution.py:446
  134.1 37.3 %collective-permute-start.15 = (bf16[256,2816]{1,0:T(8,128)(2,1)}, bf16[256,2816]{1,0:T(8,128)(2,1)}, u32[]{:S(2)}, u32[]{:S(2)}) collective-permute-start(bf16[256,2816]{1,0:T(8,128)(2,1)} %collective-permute-done.10), channel_id=1, source_target_pairs={{0,16},{8,24},{16,0},{24,8},{1,17},{9,25},{17,1},{25,9},{2,18},{10... | collective-permute-start | bytes 4325384 | tf_op jit(solution)/shard_map/ppermute | solution.py:287
  202.7 107.0 %all-gather.9.cloned.1.call-start = ((), (), s32[]{:S(2)}) async-start(), calls=%async_computation.7 | async-start | bytes 3276800 | tf_op jit(solution)/shard_map/all_gather | solution.py:442
  256.0 155.7 %reduce-scatter.7.cloned.1.call-start = ((), (), s32[]{:S(2)}) async-start(), calls=%async_computation.8 | async-start | bytes 3276800 | tf_op jit(solution)/shard_map/reduce_scatter | solution.py:446
  335.2 77.8 %collective-permute-start.19 = (bf16[2048,1408]{1,0:T(8,128)(2,1)}, bf16[2048,1408]{1,0:T(8,128)(2,1)}, u32[]{:S(2)}, u32[]{:S(2)}) collective-permute-start(bf16[2048,1408]{1,0:T(8,128)(2,1)} %convolution_convert_fusion), channel_id=1, source_target_pairs={{0,8},{8,0},{16,24},{24,16},{1,9},{9,1},{17,25},{25,17},{2,10},{10... | collective-permute-start | bytes 17301512 | tf_op jit(solution)/shard_map/ppermute | solution.py:287
  344.7 149.9 %all-gather.11.cloned.1.call-start = ((), (), s32[]{:S(2)}) async-start(), calls=%async_computation.9 | async-start | bytes 3276800 | tf_op jit(solution)/shard_map/all_gather | solution.py:442
  353.5 33.7 %collective-permute-start.20 = (bf16[1408,512]{1,0:T(8,128)(2,1)}, bf16[1408,512]{1,0:T(8,128)(2,1)S(1)}, u32[]{:S(2)}, u32[]{:S(2)}) collective-permute-start(bf16[1408,512]{1,0:T(8,128)(2,1)} %slice.310), channel_id=1, source_target_pairs={{0,4},{4,0},{1,5},{5,1},{2,6},{6,2},{3,7},{7,3},{8,12},{12,8},{9,1... | collective-permute-start | bytes 4325384 | tf_op jit(solution)/shard_map/ppermute | solution.py:284
  423.4 62.8 %collective-permute-start.21 = (bf16[1024,1408]{1,0:T(8,128)(2,1)}, bf16[1024,1408]{1,0:T(8,128)(2,1)}, u32[]{:S(2)}, u32[]{:S(2)}) collective-permute-start(bf16[1024,1408]{1,0:T(8,128)(2,1)} %slice.309), channel_id=1, source_target_pairs={{0,4},{4,0},{1,5},{5,1},{2,6},{6,2},{3,7},{7,3},{8,12},{12,8},{9,1... | collective-permute-start | bytes 8650760 | tf_op jit(solution)/shard_map/ppermute | solution.py:284
  426.8 286.3 %reduce-scatter.11.cloned.1.call-start = ((), (), s32[]{:S(2)}) async-start(), calls=%async_computation.11 | async-start | bytes 3276800 | tf_op jit(solution)/shard_map/reduce_scatter | solution.py:446
  494.0 31.0 %collective-permute-start.26 = (bf16[512,1408]{1,0:T(8,128)(2,1)}, bf16[512,1408]{1,0:T(8,128)(2,1)}, u32[]{:S(2)}, u32[]{:S(2)}) collective-permute-start(bf16[512,1408]{1,0:T(8,128)(2,1)} %dynamic-slice_convert_fusion), channel_id=1, source_target_pairs={{0,16},{8,24},{16,0},{24,8},{1,17},{9,25},{17,1},{25,9},{2,18},{10... | collective-permute-start | bytes 4325384 | tf_op jit(solution)/shard_map/ppermute | solution.py:287
  503.5 25.0 %collective-permute-start.28 = (bf16[2048,256]{1,0:T(8,128)(2,1)S(1)}, bf16[2048,256]{1,0:T(8,128)(2,1)S(1)}, u32[]{:S(2)}, u32[]{:S(2)}) collective-permute-start(bf16[2048,256]{1,0:T(8,128)(2,1)S(1)} %convolution_convert_fusion.7), channel_id=1, source_target_pairs={{0,8},{8,0},{16,24},{24,16},{1,9},{9,1},{17,25},{25,17},{2,10},{10... | collective-permute-start | bytes 3145736 | tf_op jit(solution)/shard_map/ppermute | solution.py:287
  506.0 24.9 %collective-permute-start.27 = (bf16[512,1024]{1,0:T(8,128)(2,1)S(1)}, bf16[512,1024]{1,0:T(8,128)(2,1)S(1)}, u32[]{:S(2)}, u32[]{:S(2)}) collective-permute-start(bf16[512,1024]{1,0:T(8,128)(2,1)S(1)} %convolution_convert_fusion.8), channel_id=1, source_target_pairs={{0,8},{8,0},{16,24},{24,16},{1,9},{9,1},{17,25},{25,17},{2,10},{10... | collective-permute-start | bytes 3145736 | tf_op jit(solution)/shard_map/ppermute | solution.py:287
  526.7 48.8 %collective-permute-start.30 = (bf16[512,1408]{1,0:T(8,128)(2,1)S(1)}, bf16[512,1408]{1,0:T(8,128)(2,1)}, u32[]{:S(2)}, u32[]{:S(2)}) collective-permute-start(bf16[512,1408]{1,0:T(8,128)(2,1)S(1)} %add_convert_fusion), channel_id=1, source_target_pairs={{0,16},{8,24},{16,0},{24,8},{1,17},{9,25},{17,1},{25,9},{2,18},{10... | collective-permute-start | bytes 4325384 | tf_op jit(solution)/shard_map/ppermute | solution.py:287
  594.4 122.5 %reduce-scatter.9.cloned.1.call-start = ((), (), s32[]{:S(2)}) async-start(), calls=%async_computation.10 | async-start | bytes 3276800 | tf_op jit(solution)/shard_map/reduce_scatter | solution.py:446
  620.9 110.1 %collective-permute-start.66 = (bf16[1024,1408]{1,0:T(8,128)(2,1)}, bf16[1024,1408]{1,0:T(8,128)(2,1)}, u32[]{:S(2)}, u32[]{:S(2)}) collective-permute-start(bf16[1024,1408]{1,0:T(8,128)(2,1)} %pad_maximum_fusion.8), channel_id=1, source_target_pairs={{0,8},{8,0},{16,24},{24,16},{1,9},{9,1},{17,25},{25,17},{2,10},{10... | collective-permute-start | bytes 8650760 | tf_op jit(solution)/shard_map/ppermute | solution.py:287
  648.8 23.5 %collective-permute-start.48 = (bf16[1024,256]{1,0:T(8,128)(2,1)S(1)}, bf16[1024,256]{1,0:T(8,128)(2,1)S(1)}, u32[]{:S(2)}, u32[]{:S(2)}) collective-permute-start(bf16[1024,256]{1,0:T(8,128)(2,1)S(1)} %slice.312), channel_id=1, source_target_pairs={{0,4},{4,0},{1,5},{5,1},{2,6},{6,2},{3,7},{7,3},{8,12},{12,8},{9,1... | collective-permute-start | bytes 1572872 | tf_op jit(solution)/shard_map/ppermute | solution.py:284
  650.6 32.2 %collective-permute-start.53 = (bf16[1024,256]{1,0:T(8,128)(2,1)S(1)}, bf16[1024,256]{1,0:T(8,128)(2,1)S(1)}, u32[]{:S(2)}, u32[]{:S(2)}) collective-permute-start(bf16[1024,256]{1,0:T(8,128)(2,1)S(1)} %slice.311), channel_id=1, source_target_pairs={{0,4},{4,0},{1,5},{5,1},{2,6},{6,2},{3,7},{7,3},{8,12},{12,8},{9,1... | collective-permute-start | bytes 1572872 | tf_op jit(solution)/shard_map/ppermute | solution.py:284
  661.2 22.5 %collective-permute-start.44 = (bf16[512,256]{1,0:T(8,128)(2,1)S(1)}, bf16[512,256]{1,0:T(8,128)(2,1)S(1)}, u32[]{:S(2)}, u32[]{:S(2)}) collective-permute-start(bf16[512,256]{1,0:T(8,128)(2,1)S(1)} %dynamic-slice_convert_fusion.6), channel_id=1, source_target_pairs={{0,16},{8,24},{16,0},{24,8},{1,17},{9,25},{17,1},{25,9},{2,18},{10... | collective-permute-start | bytes 786440 | tf_op jit(solution)/shard_map/ppermute | solution.py:287
  726.3 40.6 %collective-permute-start.35 = (bf16[160,1024]{1,0:T(8,128)(2,1)S(1)}, bf16[160,1024]{1,0:T(8,128)(2,1)S(1)}, u32[]{:S(2)}, u32[]{:S(2)}) collective-permute-start(bf16[160,1024]{1,0:T(8,128)(2,1)S(1)} %get-tuple-element.150), channel_id=1, source_target_pairs={{0,0},{2,1},{4,2},{6,3},{1,4},{3,5},{5,6},{7,7},{8,8},{10,9},{12,1... | collective-permute-start | bytes 983048 | tf_op jit(solution)/shard_map/ppermute | solution.py:328
  729.8 35.3 %collective-permute-start.41 = (f32[4608]{0:T(1024)S(1)}, f32[4608]{0:T(1024)S(1)}, u32[]{:S(2)}, u32[]{:S(2)}) collective-permute-start(f32[4608]{0:T(1024)S(1)} %add.434), channel_id=1, source_target_pairs={{0,2},{1,3},{2,0},{3,1},{4,6},{5,7},{6,4},{7,5},{8,10},{9,11},{10,... | collective-permute-start | bytes 55304 | tf_op jit(solution)/shard_map/ppermute | solution.py:287
  738.1 49.4 %collective-permute-start.22 = (bf16[160,1024]{1,0:T(8,128)(2,1)S(1)}, bf16[160,1024]{1,0:T(8,128)(2,1)S(1)}, u32[]{:S(2)}, u32[]{:S(2)}) collective-permute-start(bf16[160,1024]{1,0:T(8,128)(2,1)S(1)} %get-tuple-element.187), channel_id=1, source_target_pairs={{0,0},{2,1},{4,2},{6,3},{1,4},{3,5},{5,6},{7,7},{8,8},{10,9},{12,1... | collective-permute-start | bytes 983048 | tf_op jit(solution)/shard_map/ppermute | solution.py:328
  742.3 45.3 %collective-permute-start.23 = (bf16[160,1024]{1,0:T(8,128)(2,1)S(1)}, bf16[160,1024]{1,0:T(8,128)(2,1)S(1)}, u32[]{:S(2)}, u32[]{:S(2)}) collective-permute-start(bf16[160,1024]{1,0:T(8,128)(2,1)S(1)} %get-tuple-element.188), channel_id=1, source_target_pairs={{1,0},{3,1},{5,2},{7,3},{0,4},{2,5},{4,6},{6,7},{9,8},{11,9},{13,1... | collective-permute-start | bytes 983048 | tf_op jit(solution)/shard_map/ppermute | solution.py:328
  743.1 43.1 %collective-permute-start.36 = (bf16[160,1024]{1,0:T(8,128)(2,1)S(1)}, bf16[160,1024]{1,0:T(8,128)(2,1)S(1)}, u32[]{:S(2)}, u32[]{:S(2)}) collective-permute-start(bf16[160,1024]{1,0:T(8,128)(2,1)S(1)} %get-tuple-element.149), channel_id=1, source_target_pairs={{1,0},{3,1},{5,2},{7,3},{0,4},{2,5},{4,6},{6,7},{9,8},{11,9},{13,1... | collective-permute-start | bytes 983048 | tf_op jit(solution)/shard_map/ppermute | solution.py:328
  (148 other events, 1439.7 us)
Sparse Core Ops, SparseCore 0:
  31.4 62.6 all-gather.4
  103.4 52.1 all-gather.6
  202.8 50.6 reduce-scatter.4
  256.2 53.5 all-gather.8
  344.8 51.8 reduce-scatter.6
  427.0 52.6 all-gather.10
  594.5 51.0 reduce-scatter.10
  647.9 51.7 reduce-scatter.8
